TPU v7x, 32 devices: a whole 2x2x4 slice. The times are simulated.
32 devices in a mesh: depth: 2 (over y), tile: 16 (over z, x, core).
Axes of the slice: x: 2, y: 2, z: 4, core: 2. Of those that a mesh axis runs over, the one named last changes fastest.
Arguments:
- density: float32 [2, 128, 4096], P('depth', None, 'tile'), may hold values from 0.5 to 2
- prior: float32 [2, 128, 4096], P('depth', None, 'tile'), may hold values from 0.5 to 2
- observed: float32 [6, 128, 4096], P(None, None, 'tile'), may hold values from -6 to 6
- filter_across: float32 [2, 6, 4, 33], P('depth'), may hold values from -1 to 1
- filter_along: float32 [2, 6, 4, 33], P('depth'), may hold values from -0.375 to 0.375
- comp_weight: float32 [6], replicated, may hold values from 0.5 to 2
Outputs:
- gradient: float32 [2, 128, 4096], P('depth', None, 'tile')
- residual: float32 [6, 128, 4096], P(None, 'depth', 'tile')
All inputs are finite; a program needn't handle non-finite values.
Results may differ from a plain program's by a relative error of at most 0.0001.
Values sent between devices are 32-bit elements; how exact they have to be, the bound alone decides.
No kernel may reach another device: no remote copies, remote signals or barrier semaphores. Data moves between devices by JAX's collectives and lax.ppermute only.
A program may use at most 128 MiB of HBM per device.

v0:
```python
import jax
import jax.numpy as jnp
from jax import lax
from jax.experimental import pallas as pl
from jax.experimental.pallas import tpu as pltpu
from jax.sharding import PartitionSpec as P

COMPS = 6
RANK = 4
TAPS = 33
MARGIN = 16
HALO = 32
BLOCK = 32
LANES = 128
FILTERS = COMPS * RANK
ALONG_AT = 64
PRIOR_WEIGHT = 0.5
F32 = jnp.float32
BF16 = jnp.bfloat16
VMEM = pl.BlockSpec(memory_space=pltpu.VMEM)
HBM = pl.BlockSpec(memory_space=pltpu.HBM)
SMEM = pl.BlockSpec(memory_space=pltpu.SMEM)


def split(x):
    hi = x.astype(BF16)
    return hi, (x - hi.astype(F32)).astype(BF16)


def in_hbm(*arrays):
    return [pltpu.with_memory_space_constraint(x, pltpu.HBM) for x in arrays]


def limit(mib):
    return pltpu.CompilerParams(vmem_limit_bytes=mib << 20)


def pack_kernel(d_hbm, o_hbm, fa_hbm, fl_hbm, body_ref, e_ref, o_ref, d, o, fa, fl, sems):
    copies = [pltpu.make_async_copy(a, b, sems.at[i]) for i, (a, b) in enumerate(((d_hbm, d), (fa_hbm, fa), (fl_hbm, fl), (o_hbm, o)))]
    for copy in copies:
        copy.start()
    width = d.shape[2]
    even = lax.rem(lax.axis_index("tile"), 2) == 0
    for copy in copies[:3]:
        copy.wait()
    turned = d[0].T
    body_ref[0:width, :] = turned
    first, last = turned[0:HALO], turned[width - HALO : width]
    e_ref[0:HALO, :] = jnp.where(even, last, first)
    o_ref[0:HALO, :] = jnp.where(even, first, last)
    body_ref[width : width + FILTERS, :] = jnp.zeros((FILTERS, LANES), F32)
    for c in range(COMPS):
        rows = slice(width + RANK * c, width + RANK * (c + 1))
        body_ref[rows, 0:TAPS] = fa[0, c]
        body_ref[rows, ALONG_AT : ALONG_AT + TAPS] = fl[0, c]
    copies[3].wait()
    for c in range(COMPS):
        first = o[c, :, 0:LANES].T[0:MARGIN]
        last = o[c, :, width - LANES : width].T[LANES - MARGIN : LANES]
        rows = slice(HALO + MARGIN * c, HALO + MARGIN * (c + 1))
        e_ref[rows, :] = jnp.where(even, last, first)
        o_ref[rows, :] = jnp.where(even, first, last)


def pack(density, observed, across, along):
    width = density.shape[2]
    message = HALO + COMPS * MARGIN
    return pl.pallas_call(
        pack_kernel,
        out_shape=[
            jax.ShapeDtypeStruct((width + FILTERS, LANES), F32),
            jax.ShapeDtypeStruct((message, LANES), F32),
            jax.ShapeDtypeStruct((message, LANES), F32),
        ],
        in_specs=[HBM] * 4,
        out_specs=[VMEM] * 3,
        scratch_shapes=[pltpu.VMEM(x.shape, F32) for x in (density, observed, across, along)] + [pltpu.SemaphoreType.DMA((4,))],
        compiler_params=limit(8),
        name="pack",
    )(*in_hbm(density, observed, across, along))


def place(filters, first_tap, targets):
    tap = lax.broadcasted_iota(jnp.int32, (LANES, LANES), 0) - first_tap
    lane = lax.broadcasted_iota(jnp.int32, (LANES, LANES), 1)
    chosen = jnp.zeros((LANES, LANES), jnp.bool_)
    for target in targets(tap):
        chosen = chosen | (lane == target)
    chosen = (chosen & (tap >= 0) & (tap < TAPS)).astype(BF16)
    return [jnp.dot(v, chosen, preferred_element_type=F32) for v in split(filters)]


def along_blocks(base, filters, targets, dst):
    for p, placed in enumerate(place(filters, ALONG_AT, targets)):
        base[p] = placed
    for f in range(FILTERS):
        for p in range(2):
            v = jnp.broadcast_to(base[p, f : f + 1, :], (BLOCK, LANES))
            v = pltpu.roll(v, 0, 1, stride=1, stride_axis=0)
            dst[BLOCK * f : BLOCK * (f + 1), LANES * p : LANES * (p + 1)] = v.astype(BF16)


def across_blocks(base, filters, targets, dst):
    for p, placed in enumerate(place(filters, 0, targets)):
        base[p] = placed
    row = lax.broadcasted_iota(jnp.int32, (LANES, LANES), 0)
    lane = lax.broadcasted_iota(jnp.int32, (LANES, LANES), 1)
    band = jnp.abs(row - lane) <= MARGIN
    for f in range(FILTERS):
        for p in range(2):
            v = jnp.broadcast_to(base[p, f : f + 1, :], (LANES, LANES))
            v = pltpu.roll(v, 0, 1, stride=1, stride_axis=0)
            dst[LANES * f : LANES * (f + 1), LANES * p : LANES * (p + 1)] = jnp.where(band, v, 0.0).astype(BF16)


def forward_tables(base, filters, tf, zf):
    along_blocks(base, filters, lambda k: (k, k + 64), tf)
    across_blocks(base, filters, lambda k: ((MARGIN - k) & (LANES - 1),), zf)


def stacked(windows):
    columns = [jnp.concatenate([hi, lo, hi, lo], axis=0) for hi, lo in windows]
    return jnp.concatenate(columns, axis=1) if len(columns) > 1 else columns[0]


def smooth(table, windows, stores):
    hi, lo = split(jnp.dot(table, stacked(windows), preferred_element_type=F32))
    for i, store in enumerate(stores):
        for f in range(table.shape[0] // BLOCK):
            part = (slice(BLOCK * f, BLOCK * (f + 1)), slice(LANES * i, LANES * (i + 1)))
            store(f, hi[part], lo[part])


def into(shi, slo, row):
    def store(f, hi, lo):
        c, r = divmod(f, RANK)
        at = (c, slice(row, row + BLOCK), slice(LANES * r, LANES * (r + 1)))
        shi[at] = hi
        slo[at] = lo

    return store


def smooth_inside(body_ref, dhi, dlo, tf, shi, slo):
    width = dhi.shape[0]
    dhi[...], dlo[...] = split(body_ref[0:width, :])
    inside = width // BLOCK - 1
    window = lambda b: (dhi[BLOCK * b : BLOCK * b + 64, :], dlo[BLOCK * b : BLOCK * b + 64, :])
    for b in range(0, inside, 2):
        group = range(b, min(b + 2, inside))
        smooth(tf[...], [window(i) for i in group], [into(shi, slo, BLOCK * i) for i in group])


def own_kernel(body_ref, o_hbm, tf, zf, tb, zb, shi, slo, obst, dhi, dlo, base, o, sem):
    copy = pltpu.make_async_copy(o_hbm, o, sem)
    copy.start()
    width = dhi.shape[0]
    filters = body_ref[width : width + FILTERS, :]
    forward_tables(base, filters, tf, zf)
    smooth_inside(body_ref, dhi, dlo, tf, shi, slo)
    along_blocks(base, filters, lambda k: (TAPS - 1 - k, TAPS - 1 - k + 64), tb)
    across_blocks(base, filters, lambda k: ((k - MARGIN) & (LANES - 1),), zb)
    copy.wait()
    for c in range(COMPS):
        obst[c] = o[c].T


def other_kernel(body_ref, tf, zf, shi, slo, dhi, dlo, base):
    width = dhi.shape[0]
    forward_tables(base, body_ref[width : width + FILTERS, :], tf, zf)
    smooth_inside(body_ref, dhi, dlo, tf, shi, slo)


def tables(width):
    along = jax.ShapeDtypeStruct((FILTERS * BLOCK, 2 * LANES), BF16)
    across = jax.ShapeDtypeStruct((FILTERS * LANES, 2 * LANES), BF16)
    smoothed = jax.ShapeDtypeStruct((COMPS, width - BLOCK, RANK * LANES), BF16)
    scratch = [pltpu.VMEM((width, LANES), BF16)] * 2 + [pltpu.VMEM((2, FILTERS, LANES), F32)]
    return along, across, smoothed, scratch


def own_part(sent, observed):
    width = observed.shape[2]
    along, across, smoothed, scratch = tables(width)
    out = [along, across, along, across, smoothed, smoothed, jax.ShapeDtypeStruct((COMPS, width, LANES), F32)]
    return pl.pallas_call(
        own_kernel,
        out_shape=out,
        in_specs=[VMEM, HBM],
        out_specs=[VMEM] * len(out),
        scratch_shapes=scratch + [pltpu.VMEM(observed.shape, F32), pltpu.SemaphoreType.DMA],
        compiler_params=limit(8),
        cost_estimate=pl.CostEstimate(flops=2_000_000_000, bytes_accessed=4_000_000, transcendentals=0),
        name="own",
    )(sent, *in_hbm(observed))


def other_part(received):
    width = received.shape[0] - FILTERS
    along, across, smoothed, scratch = tables(width)
    return pl.pallas_call(
        other_kernel,
        out_shape=[along, across, smoothed, smoothed],
        in_specs=[VMEM],
        out_specs=[VMEM] * 4,
        scratch_shapes=scratch,
        compiler_params=limit(8),
        cost_estimate=pl.CostEstimate(flops=2_000_000_000, bytes_accessed=4_000_000, transcendentals=0),
        name="other",
    )(received)


def final_kernel(layers, *refs):
    it = iter(refs)
    take = lambda k: [next(it) for _ in range(k)]
    d_hbm, p_hbm, w_ref, e_ref, o_ref, tb, zb, obst = take(8)
    bodies, tfs, zfs, shis, slos = (take(layers) for _ in range(5))
    halos = take(layers - 1)
    grad_hbm, res_hbm = take(2)
    ehi, elo, rhi, rlo, bhi, blo, turned, res, d, p, grad, sems = take(12)
    copy_d = pltpu.make_async_copy(d_hbm, d, sems.at[0])
    copy_p = pltpu.make_async_copy(p_hbm, p, sems.at[1])
    copy_d.start()
    copy_p.start()
    tile, tiles = lax.axis_index("tile"), lax.axis_size("tile")
    even = lax.rem(tile, 2) == 0
    has_left, has_right = tile > 0, tile < tiles - 1
    width = obst.shape[1]
    share = res.shape[1]
    padded = width + 2 * MARGIN
    for l in range(layers):
        from_e = e_ref[0:HALO, :] if l == 0 else halos[l - 1][0:HALO, :]
        from_o = o_ref[0:HALO, :] if l == 0 else halos[l - 1][HALO : 2 * HALO, :]
        left = jnp.where(has_left, jnp.where(even, from_o, from_e), 0.0)
        right = jnp.where(has_right, jnp.where(even, from_e, from_o), 0.0)
        windows = [
            split(jnp.concatenate([left, bodies[l][0:HALO, :]], axis=0)),
            split(jnp.concatenate([bodies[l][width - HALO : width, :], right], axis=0)),
        ]
        smooth(tfs[l][...], windows, [into(ehi.at[l], elo.at[l], 0), into(ehi.at[l], elo.at[l], BLOCK)])

    first_row = lax.axis_index("depth") * share
    for c in range(COMPS):
        lhs, rhs = [], []
        for edge, inside in ((ehi, shis), (elo, slos)):
            for l in range(layers):
                lhs.append(jnp.concatenate([edge[l, c, 0:BLOCK, :], inside[l][c], edge[l, c, BLOCK : 2 * BLOCK, :]], axis=0))
                rhs.append(zfs[l][RANK * LANES * c : RANK * LANES * (c + 1), :])
        out = jnp.dot(jnp.concatenate(lhs, axis=1), jnp.concatenate(rhs, axis=0), preferred_element_type=F32)
        response = out[:, 0:LANES] + out[:, LANES : 2 * LANES]
        w = w_ref[c]
        center = (response[MARGIN : MARGIN + width] - obst[c]) * w
        rows = slice(HALO + MARGIN * c, HALO + MARGIN * (c + 1))
        left = jnp.where(even, o_ref[rows, :], e_ref[rows, :])
        right = jnp.where(even, e_ref[rows, :], o_ref[rows, :])
        left = jnp.where(has_left, (response[0:MARGIN] - left) * w, 0.0)
        right = jnp.where(has_right, (response[MARGIN + width : padded] - right) * w, 0.0)
        for at, part in ((0, left), (MARGIN, center), (MARGIN + width, right)):
            hi, lo = split(part)
            rhi[c, at : at + part.shape[0], :] = hi
            rlo[c, at : at + part.shape[0], :] = lo
        turned[c] = center.T
        res[c] = turned[c, pl.ds(first_row, share), :]
    copy_res = pltpu.make_async_copy(res, res_hbm, sems.at[2])
    copy_res.start()

    for c in range(COMPS):
        window = lambda b: (rhi[c, BLOCK * b : BLOCK * b + 64, :], rlo[c, BLOCK * b : BLOCK * b + 64, :])

        def store(b):
            def put(r, hi, lo):
                at = (slice(BLOCK * b, BLOCK * (b + 1)), slice(LANES * (RANK * c + r), LANES * (RANK * c + r + 1)))
                bhi[at] = hi
                blo[at] = lo

            return put

        table = tb[RANK * BLOCK * c : RANK * BLOCK * (c + 1), :]
        for b in range(0, width // BLOCK, 2):
            smooth(table, [window(b), window(b + 1)], [store(b), store(b + 1)])
    z = zb[...]
    out = jnp.dot(jnp.concatenate([bhi[...], blo[...]], axis=1), jnp.concatenate([z, z], axis=0), preferred_element_type=F32)
    adjoint = (out[:, 0:LANES] + out[:, LANES : 2 * LANES]).T
    copy_d.wait()
    copy_p.wait()
    grad[0] = adjoint + PRIOR_WEIGHT * (jnp.log(d[0]) - jnp.log(p[0]))
    copy_grad = pltpu.make_async_copy(grad, grad_hbm, sems.at[3])
    copy_grad.start()
    copy_res.wait()
    copy_grad.wait()


def final_part(layers, density, prior, weight, e, o, tb, zb, obst, bodies, tfs, zfs, shis, slos, halos):
    rows, width = density.shape[1:]
    share = rows // layers
    padded = width + 2 * MARGIN
    args = [*in_hbm(density, prior), weight, e, o, tb, zb, obst, *bodies, *tfs, *zfs, *shis, *slos, *halos]
    return pl.pallas_call(
        lambda *refs: final_kernel(layers, *refs),
        out_shape=[jax.ShapeDtypeStruct((1, rows, width), F32), jax.ShapeDtypeStruct((COMPS, share, width), F32)],
        in_specs=[HBM, HBM, SMEM] + [VMEM] * (len(args) - 3),
        out_specs=[HBM, HBM],
        scratch_shapes=[
            *[pltpu.VMEM((layers, COMPS, 2 * BLOCK, RANK * LANES), BF16)] * 2,
            *[pltpu.VMEM((COMPS, padded, LANES), BF16)] * 2,
            *[pltpu.VMEM((width, FILTERS * LANES), BF16)] * 2,
            pltpu.VMEM((COMPS, rows, width), F32),
            pltpu.VMEM((COMPS, share, width), F32),
            *[pltpu.VMEM((1, rows, width), F32)] * 3,
            pltpu.SemaphoreType.DMA((4,)),
        ],
        compiler_params=limit(12 + 2 * layers),
        name="final",
    )(*args)


def body(density, prior, observed, filter_across, filter_along, comp_weight):
    layers, tiles = lax.axis_size("depth"), lax.axis_size("tile")
    both = ("depth", "tile")
    at = lambda d, t: d * tiles + t
    inner = [(i, i ^ 1) for i in range(tiles)]
    outer = [(at(d, i), at(d, i + 1)) for d in range(layers) for i in range(1, tiles - 1, 2)]
    outer += [(j, i) for i, j in outer]
    outer += [(at(d, t), at(d ^ 1, t)) for d in range(layers) for t in (0, tiles - 1)]
    turns = [[(d, (d + s) % layers) for d in range(layers)] for s in range(1, layers)]

    sent, e, o = pack(density, observed, filter_across, filter_along)
    bodies = [sent] + [lax.ppermute(sent, "depth", turn) for turn in turns]
    from_e = lax.ppermute(e, "tile", inner)
    from_o = lax.ppermute(o, both, outer)
    tf, zf, tb, zb, shi, slo, obst = own_part(sent, observed)
    halo = jnp.concatenate([from_e[0:HALO], from_o[0:HALO]], axis=0)
    halo, _ = lax.optimization_barrier((halo, obst))
    halos = [lax.ppermute(halo, "depth", turn) for turn in turns]
    others = [other_part(received) for received in bodies[1:]]
    tfs, zfs, shis, slos = ([first] + [x[i] for x in others] for i, first in enumerate((tf, zf, shi, slo)))
    return tuple(
        final_part(layers, density, prior, comp_weight, from_e, from_o, tb, zb, obst, bodies, tfs, zfs, shis, slos, halos)
    )


def solution(mesh):
    placed = (
        P("depth", None, "tile"),
        P("depth", None, "tile"),
        P(None, None, "tile"),
        P("depth", None, None, None),
        P("depth", None, None, None),
        P(),
    )
    return jax.shard_map(
        body,
        mesh=mesh,
        in_specs=placed,
        out_specs=(P("depth", None, "tile"), P(None, "depth", "tile")),
        check_vma=False,
    )
```

profile of v0, /device:TPU:0, one launch (start us, length us, event | category | flops | bytes accessed | tf_op | source)
XLA Modules:
  0.0 19.5 jit_solution(1983243635362516458)
XLA Ops:
  0.6 1.6 %pack.1 = (f32[280,128]{1,0:T(8,128)S(1)}, f32[128,128]{1,0:T(8,128)S(1)}, f32[128,128]{1,0:T(8,128)S(1)}) custom-call(f32[1,128,256]{2,1,0:T(8,128)} %refs_0_.1, f32[6,128,256]{2,1,0:T(8,128)} %o_hbm.3, f32[1,6,4,33]{3,2,1,0:T(4,128)} %fa_hbm.1, f32[1,6,4,33]{3,2,1,0:T(4,128)} %fl_hbm.1), custom_call_target="tpu_custom_call" | custom-call | tf_op jit(solution)/shard_map/pack/pallas_call | solution.py:68
  2.2 0.5 %collective-permute-start = (f32[128,128]{1,0:T(8,128)S(1)}, f32[128,128]{1,0:T(8,128)S(1)}, u32[]{:S(2)}, u32[]{:S(2)}) collective-permute-start(f32[128,128]{1,0:T(8,128)S(1)} %get-tuple-element.17), channel_id=1, source_target_pairs={{0,1},{1,0},{2,3},{3,2},{4,5},{5,4},{6,7},{7,6},{8,9},{9,8},{10,11... | collective-permute-start | bytes 196616 | tf_op jit(solution)/shard_map/ppermute | solution.py:329
  2.7 2.6 %collective-permute-start.1 = (f32[128,128]{1,0:T(8,128)S(1)}, f32[128,128]{1,0:T(8,128)S(1)}, u32[]{:S(2)}, u32[]{:S(2)}) collective-permute-start(f32[128,128]{1,0:T(8,128)S(1)} %get-tuple-element.18), channel_id=1, source_target_pairs={{1,2},{3,4},{5,6},{7,8},{9,10},{11,12},{13,14},{17,18},{19,20},{21... | collective-permute-start | bytes 196616 | tf_op jit(solution)/shard_map/ppermute | solution.py:330
  5.3 0.1 collective-permute-start.2
  5.4 2.6 %own.1 = (bf16[768,256]{1,0:T(8,128)(2,1)S(1)}, bf16[3072,256]{1,0:T(8,128)(2,1)S(1)}, bf16[768,256]{1,0:T(8,128)(2,1)S(1)}, bf16[3072,256]{1,0:T(8,128)(2,1)S(1...) custom-call(f32[280,128]{1,0:T(8,128)S(1)} %get-tuple-element.19.body_ref.refs_8_,, ...), custom_call_target="tpu_custom_call" | custom-call | flops 2000000000 | bytes 4000000 | tf_op jit(solution)/shard_map/own/pallas_call | solution.py:186
  7.9 0.0 collective-permute-done.refs_3_
  8.0 0.0 collective-permute-done.1.refs_4_
  8.0 0.0 copy-start
  8.0 2.0 %collective-permute-start.3 = (f32[64,128]{1,0:T(8,128)S(1)}, f32[64,128]{1,0:T(8,128)S(1)}, u32[]{:S(2)}, u32[]{:S(2)}) collective-permute-start(f32[64,128]{1,0:T(8,128)S(1)} %pad_maximum_fusion), channel_id=1, source_target_pairs={{0,16},{16,0},{1,17},{17,1},{2,18},{18,2},{3,19},{19,3},{4,20},{20... | collective-permute-start | bytes 98312 | tf_op jit(solution)/shard_map/ppermute | solution.py:334
  10.0 1.0 %collective-permute-done.2.body_ref.refs_9_ = f32[280,128]{1,0:T(8,128)S(1)} collective-permute-done((f32[280,128]{1,0:T(8,128)S(1)}, f32[280,128]{1,0:T(8,128)S(1)}, u32[]{:S(2)}, u32[]{:S(2)}) %collective-permute-start.2) | collective-permute-done | bytes 143392 | tf_op jit(solution)/shard_map/ppermute | solution.py:328
  11.1 1.1 %other.1 = (bf16[768,256]{1,0:T(8,128)(2,1)S(1)}, bf16[3072,256]{1,0:T(8,128)(2,1)S(1)}, bf16[6,224,512]{2,1,0:T(8,128)(2,1)S(1)}, bf16[6,224,512]{2,1,0:T(8,128)(2,1)S(1)}) custom-call(f32[280,128]{1,0:T(8,128)S(1)} %collective-permute-done.2.body_ref.refs_9_), custom_call_target="tpu_custom_call" | custom-call | flops 2000000000 | bytes 4000000 | tf_op jit(solution)/shard_map/other/pallas_call | solution.py:201
  12.2 0.0 collective-permute-done.3.refs_18_
  12.2 0.0 copy-done
  12.2 7.2 %final.1 = (f32[1,128,256]{2,1,0:T(8,128)}, f32[6,64,256]{2,1,0:T(8,128)}) custom-call(f32[1,128,256]{2,1,0:T(8,128)} %refs_0_.1, f32[1,128,256]{2,1,0:T(8,128)} %refs_1_.1, f32[6]{0:T(128)S(1)} %copy-done, f32[128,128]{1,0:T(8,128)S(1)} %collective-permute-done.refs_3_, f32[128,128]{1,0:T(8,128)S(1)} %collective-permute-done.1.refs_4_, ...), custom_call_target="tpu_custom_call" | custom-call | tf_op jit(solution)/shard_map/final/pallas_call | solution.py:298
  (3 shorter events, 0.0 us)
Async XLA Ops:
  2.2 5.8 %collective-permute-start = (f32[128,128]{1,0:T(8,128)S(1)}, f32[128,128]{1,0:T(8,128)S(1)}, u32[]{:S(2)}, u32[]{:S(2)}) collective-permute-start(f32[128,128]{1,0:T(8,128)S(1)} %get-tuple-element.17), channel_id=1, source_target_pairs={{0,1},{1,0},{2,3},{3,2},{4,5},{5,4},{6,7},{7,6},{8,9},{9,8},{10,11... | collective-permute-start | bytes 196616 | tf_op jit(solution)/shard_map/ppermute | solution.py:329
  2.7 5.3 %collective-permute-start.1 = (f32[128,128]{1,0:T(8,128)S(1)}, f32[128,128]{1,0:T(8,128)S(1)}, u32[]{:S(2)}, u32[]{:S(2)}) collective-permute-start(f32[128,128]{1,0:T(8,128)S(1)} %get-tuple-element.18), channel_id=1, source_target_pairs={{1,2},{3,4},{5,6},{7,8},{9,10},{11,12},{13,14},{17,18},{19,20},{21... | collective-permute-start | bytes 196616 | tf_op jit(solution)/shard_map/ppermute | solution.py:330
  5.3 5.8 %collective-permute-start.2 = (f32[280,128]{1,0:T(8,128)S(1)}, f32[280,128]{1,0:T(8,128)S(1)}, u32[]{:S(2)}, u32[]{:S(2)}) collective-permute-start(f32[280,128]{1,0:T(8,128)S(1)} %get-tuple-element.19.body_ref.refs_8_), channel_id=1, source_target_pairs={{0,16},{16,0},{1,17},{17,1},{2,18},{18,2},{3,19},{19,3},{4,20},{20... | collective-permute-start | bytes 430088 | tf_op jit(solution)/shard_map/ppermute | solution.py:328
  8.0 4.2 %copy-start = (f32[6]{0:T(128)S(1)}, f32[6]{0:T(128)}, u32[]{:S(2)}) copy-start(f32[6]{0:T(128)} %refs_2_.1) | copy-start | bytes 76
  8.0 4.2 %collective-permute-start.3 = (f32[64,128]{1,0:T(8,128)S(1)}, f32[64,128]{1,0:T(8,128)S(1)}, u32[]{:S(2)}, u32[]{:S(2)}) collective-permute-start(f32[64,128]{1,0:T(8,128)S(1)} %pad_maximum_fusion), channel_id=1, source_target_pairs={{0,16},{16,0},{1,17},{17,1},{2,18},{18,2},{3,19},{19,3},{4,20},{20... | collective-permute-start | bytes 98312 | tf_op jit(solution)/shard_map/ppermute | solution.py:334
where the time goes:
time: 19.7 us; the launch traced here: 19.5 us
  Pallas kernels  12.5 us (63%)
  starting transfers between devices  5.2 us (26%)
  waiting for transfers between devices  1.04 us (5%)
  between operations  0.72 us (4%)
    pallas_call x1, Pallas kernels, final_part(): pl.pallas_call(lambda *refs: final_kernel(layers, *refs), out_shape=[jax....  7.24 us
    ppermute x1, starting transfers between devices, body(): from_o = lax.ppermute(o, both, outer)  2.59 us
    pallas_call x1, Pallas kernels, own_part(): pl.pallas_call(own_kernel, out_shape=out, in_specs=[VMEM, HBM], out_specs...  2.56 us
    ppermute x1, starting transfers between devices, body(): halos = [lax.ppermute(halo, 'depth', turn) for turn in turns]  2.01 us
    pallas_call x1, Pallas kernels, pack(): pl.pallas_call(pack_kernel, out_shape=[jax.ShapeDtypeStruct((width + FILT...  1.55 us
    pallas_call x1, Pallas kernels, other_part(): pl.pallas_call(other_kernel, out_shape=[along, across, smoothed, smoothed...  1.14 us
    ppermute x1, waiting for transfers between devices, body(): bodies = [sent] + [lax.ppermute(sent, 'depth', turn) for turn in turns]  1.03 us
    ppermute x1, starting transfers between devices, body(): from_e = lax.ppermute(e, 'tile', inner)  0.52 us
  transfers between devices with their start and end apart: 4, of which 1 were waited for; matrix products, arithmetic and copies ran while one was open for 0% of the time, Pallas kernels for 19%

commit v1 on v0

--- a/solution.py
+++ b/solution.py
@@ -35,49 +35,96 @@
     return pltpu.CompilerParams(vmem_limit_bytes=mib << 20)
 
 
-def pack_kernel(d_hbm, o_hbm, fa_hbm, fl_hbm, body_ref, e_ref, o_ref, d, o, fa, fl, sems):
-    copies = [pltpu.make_async_copy(a, b, sems.at[i]) for i, (a, b) in enumerate(((d_hbm, d), (fa_hbm, fa), (fl_hbm, fl), (o_hbm, o)))]
+def turn_kernel(d_hbm, fa_hbm, fl_hbm, o_hbm, body_ref, o_ref, d, fa, fl, sems):
+    moves = ((fa_hbm, fa), (fl_hbm, fl), (d_hbm, d), (o_hbm, o_ref))
+    copies = [pltpu.make_async_copy(a, b, sems.at[i]) for i, (a, b) in enumerate(moves)]
     for copy in copies:
         copy.start()
-    width = d.shape[2]
-    even = lax.rem(lax.axis_index("tile"), 2) == 0
     for copy in copies[:3]:
         copy.wait()
-    turned = d[0].T
-    body_ref[0:width, :] = turned
-    first, last = turned[0:HALO], turned[width - HALO : width]
-    e_ref[0:HALO, :] = jnp.where(even, last, first)
-    o_ref[0:HALO, :] = jnp.where(even, first, last)
+    width = d.shape[2]
+    body_ref[0:width, :] = d[0].T
     body_ref[width : width + FILTERS, :] = jnp.zeros((FILTERS, LANES), F32)
     for c in range(COMPS):
         rows = slice(width + RANK * c, width + RANK * (c + 1))
         body_ref[rows, 0:TAPS] = fa[0, c]
         body_ref[rows, ALONG_AT : ALONG_AT + TAPS] = fl[0, c]
     copies[3].wait()
-    for c in range(COMPS):
-        first = o[c, :, 0:LANES].T[0:MARGIN]
-        last = o[c, :, width - LANES : width].T[LANES - MARGIN : LANES]
-        rows = slice(HALO + MARGIN * c, HALO + MARGIN * (c + 1))
-        e_ref[rows, :] = jnp.where(even, last, first)
-        o_ref[rows, :] = jnp.where(even, first, last)
-
-
-def pack(density, observed, across, along):
-    width = density.shape[2]
-    message = HALO + COMPS * MARGIN
-    return pl.pallas_call(
-        pack_kernel,
+
+
+def turn(density, across, along, observed):
+    return pl.pallas_call(
+        turn_kernel,
         out_shape=[
-            jax.ShapeDtypeStruct((width + FILTERS, LANES), F32),
-            jax.ShapeDtypeStruct((message, LANES), F32),
-            jax.ShapeDtypeStruct((message, LANES), F32),
+            jax.ShapeDtypeStruct((density.shape[2] + FILTERS, LANES), F32),
+            jax.ShapeDtypeStruct(observed.shape, F32),
         ],
         in_specs=[HBM] * 4,
+        out_specs=[VMEM] * 2,
+        scratch_shapes=[pltpu.VMEM(x.shape, F32) for x in (density, across, along)] + [pltpu.SemaphoreType.DMA((4,))],
+        compiler_params=limit(4),
+        name="turn",
+    )(*in_hbm(density, across, along, observed))
+
+
+def is_even():
+    return lax.rem(lax.axis_index("tile"), 2) == 0
+
+
+def outer_edge(x):
+    return jnp.where(is_even(), x[0:HALO, :], x[x.shape[0] - HALO : x.shape[0], :])
+
+
+def inner_edge(x):
+    return jnp.where(is_even(), x[x.shape[0] - HALO : x.shape[0], :], x[0:HALO, :])
+
+
+def outer_kernel(body_ref, o_ref, out_ref, od_ref, in_ref):
+    width = o_ref.shape[2]
+    even = is_even()
+    edge = outer_edge(body_ref.at[0:width])
+    out_ref[0:HALO, :] = edge
+    od_ref[...] = edge
+    for c in range(COMPS):
+        first = o_ref[c, :, 0:LANES].T[0:MARGIN]
+        last = o_ref[c, :, width - LANES : width].T[LANES - MARGIN : LANES]
+        out_ref[HALO + MARGIN * c : HALO + MARGIN * (c + 1), :] = jnp.where(even, first, last)
+        in_ref[MARGIN * c : MARGIN * (c + 1), :] = jnp.where(even, last, first)
+
+
+def outer_part(sent, observed):
+    return pl.pallas_call(
+        outer_kernel,
+        out_shape=[
+            jax.ShapeDtypeStruct((HALO + COMPS * MARGIN, LANES), F32),
+            jax.ShapeDtypeStruct((HALO, LANES), F32),
+            jax.ShapeDtypeStruct((COMPS * MARGIN, LANES), F32),
+        ],
+        in_specs=[VMEM] * 2,
         out_specs=[VMEM] * 3,
-        scratch_shapes=[pltpu.VMEM(x.shape, F32) for x in (density, observed, across, along)] + [pltpu.SemaphoreType.DMA((4,))],
-        compiler_params=limit(8),
-        name="pack",
-    )(*in_hbm(density, observed, across, along))
+        compiler_params=limit(4),
+        name="outer",
+    )(sent, observed)
+
+
+def inner_kernel(layers, *refs):
+    obs_ref, bodies, out_ref = refs[0], refs[1:-1], refs[-1]
+    width = bodies[0].shape[0] - FILTERS
+    for l in range(layers):
+        out_ref[HALO * l : HALO * (l + 1), :] = inner_edge(bodies[l].at[0:width])
+    out_ref[HALO * layers :, :] = obs_ref[...]
+
+
+def inner_part(edge, bodies):
+    layers = len(bodies)
+    return pl.pallas_call(
+        lambda *refs: inner_kernel(layers, *refs),
+        out_shape=jax.ShapeDtypeStruct((HALO * layers + COMPS * MARGIN, LANES), F32),
+        in_specs=[VMEM] * (1 + layers),
+        out_specs=VMEM,
+        compiler_params=limit(4),
+        name="inner",
+    )(edge, *bodies)
 
 
 def place(filters, first_tap, targets):
@@ -151,18 +198,15 @@
         smooth(tf[...], [window(i) for i in group], [into(shi, slo, BLOCK * i) for i in group])
 
 
-def own_kernel(body_ref, o_hbm, tf, zf, tb, zb, shi, slo, obst, dhi, dlo, base, o, sem):
-    copy = pltpu.make_async_copy(o_hbm, o, sem)
-    copy.start()
+def own_kernel(body_ref, o_ref, tf, zf, tb, zb, shi, slo, obst, dhi, dlo, base):
     width = dhi.shape[0]
     filters = body_ref[width : width + FILTERS, :]
     forward_tables(base, filters, tf, zf)
     smooth_inside(body_ref, dhi, dlo, tf, shi, slo)
     along_blocks(base, filters, lambda k: (TAPS - 1 - k, TAPS - 1 - k + 64), tb)
     across_blocks(base, filters, lambda k: ((k - MARGIN) & (LANES - 1),), zb)
-    copy.wait()
     for c in range(COMPS):
-        obst[c] = o[c].T
+        obst[c] = o_ref[c].T
 
 
 def other_kernel(body_ref, tf, zf, shi, slo, dhi, dlo, base):
@@ -186,13 +230,13 @@
     return pl.pallas_call(
         own_kernel,
         out_shape=out,
-        in_specs=[VMEM, HBM],
+        in_specs=[VMEM, VMEM],
         out_specs=[VMEM] * len(out),
-        scratch_shapes=scratch + [pltpu.VMEM(observed.shape, F32), pltpu.SemaphoreType.DMA],
+        scratch_shapes=scratch,
         compiler_params=limit(8),
         cost_estimate=pl.CostEstimate(flops=2_000_000_000, bytes_accessed=4_000_000, transcendentals=0),
         name="own",
-    )(sent, *in_hbm(observed))
+    )(sent, observed)
 
 
 def other_part(received):
@@ -217,20 +261,20 @@
     bodies, tfs, zfs, shis, slos = (take(layers) for _ in range(5))
     halos = take(layers - 1)
     grad_hbm, res_hbm = take(2)
-    ehi, elo, rhi, rlo, bhi, blo, turned, res, d, p, grad, sems = take(12)
+    ehi, elo, rhi, rlo, bhi, blo, turned, res, d, p, grad, acc, sems = take(13)
     copy_d = pltpu.make_async_copy(d_hbm, d, sems.at[0])
     copy_p = pltpu.make_async_copy(p_hbm, p, sems.at[1])
     copy_d.start()
     copy_p.start()
     tile, tiles = lax.axis_index("tile"), lax.axis_size("tile")
-    even = lax.rem(tile, 2) == 0
+    even = is_even()
     has_left, has_right = tile > 0, tile < tiles - 1
     width = obst.shape[1]
     share = res.shape[1]
     padded = width + 2 * MARGIN
     for l in range(layers):
-        from_e = e_ref[0:HALO, :] if l == 0 else halos[l - 1][0:HALO, :]
-        from_o = o_ref[0:HALO, :] if l == 0 else halos[l - 1][HALO : 2 * HALO, :]
+        from_e = e_ref[HALO * l : HALO * (l + 1), :]
+        from_o = o_ref[0:HALO, :] if l == 0 else halos[l - 1][...]
         left = jnp.where(has_left, jnp.where(even, from_o, from_e), 0.0)
         right = jnp.where(has_right, jnp.where(even, from_e, from_o), 0.0)
         windows = [
@@ -240,7 +284,8 @@
         smooth(tfs[l][...], windows, [into(ehi.at[l], elo.at[l], 0), into(ehi.at[l], elo.at[l], BLOCK)])
 
     first_row = lax.axis_index("depth") * share
-    for c in range(COMPS):
+
+    def forward(c):
         lhs, rhs = [], []
         for edge, inside in ((ehi, shis), (elo, slos)):
             for l in range(layers):
@@ -250,9 +295,10 @@
         response = out[:, 0:LANES] + out[:, LANES : 2 * LANES]
         w = w_ref[c]
         center = (response[MARGIN : MARGIN + width] - obst[c]) * w
-        rows = slice(HALO + MARGIN * c, HALO + MARGIN * (c + 1))
-        left = jnp.where(even, o_ref[rows, :], e_ref[rows, :])
-        right = jnp.where(even, e_ref[rows, :], o_ref[rows, :])
+        from_o = o_ref[HALO + MARGIN * c : HALO + MARGIN * (c + 1), :]
+        from_e = e_ref[HALO * layers + MARGIN * c : HALO * layers + MARGIN * (c + 1), :]
+        left = jnp.where(even, from_o, from_e)
+        right = jnp.where(even, from_e, from_o)
         left = jnp.where(has_left, (response[0:MARGIN] - left) * w, 0.0)
         right = jnp.where(has_right, (response[MARGIN + width : padded] - right) * w, 0.0)
         for at, part in ((0, left), (MARGIN, center), (MARGIN + width, right)):
@@ -261,15 +307,13 @@
             rlo[c, at : at + part.shape[0], :] = lo
         turned[c] = center.T
         res[c] = turned[c, pl.ds(first_row, share), :]
-    copy_res = pltpu.make_async_copy(res, res_hbm, sems.at[2])
-    copy_res.start()
-
-    for c in range(COMPS):
+
+    def adjoint(c):
         window = lambda b: (rhi[c, BLOCK * b : BLOCK * b + 64, :], rlo[c, BLOCK * b : BLOCK * b + 64, :])
 
         def store(b):
             def put(r, hi, lo):
-                at = (slice(BLOCK * b, BLOCK * (b + 1)), slice(LANES * (RANK * c + r), LANES * (RANK * c + r + 1)))
+                at = (c, slice(BLOCK * b, BLOCK * (b + 1)), slice(LANES * r, LANES * (r + 1)))
                 bhi[at] = hi
                 blo[at] = lo
 
@@ -278,12 +322,24 @@
         table = tb[RANK * BLOCK * c : RANK * BLOCK * (c + 1), :]
         for b in range(0, width // BLOCK, 2):
             smooth(table, [window(b), window(b + 1)], [store(b), store(b + 1)])
-    z = zb[...]
-    out = jnp.dot(jnp.concatenate([bhi[...], blo[...]], axis=1), jnp.concatenate([z, z], axis=0), preferred_element_type=F32)
-    adjoint = (out[:, 0:LANES] + out[:, LANES : 2 * LANES]).T
+        z = zb[RANK * LANES * c : RANK * LANES * (c + 1), :]
+        return jnp.dot(jnp.concatenate([bhi[c], blo[c]], axis=1), jnp.concatenate([z, z], axis=0), preferred_element_type=F32)
+
+    for c in range(COMPS + 1):
+        if c < COMPS:
+            forward(c)
+        if c == COMPS - 1:
+            copy_res = pltpu.make_async_copy(res, res_hbm, sems.at[2])
+            copy_res.start()
+        if c == 1:
+            acc[...] = adjoint(0)
+        if c > 1:
+            acc[...] += adjoint(c - 1)
+    out = acc[...]
+    adj = (out[:, 0:LANES] + out[:, LANES : 2 * LANES]).T
     copy_d.wait()
     copy_p.wait()
-    grad[0] = adjoint + PRIOR_WEIGHT * (jnp.log(d[0]) - jnp.log(p[0]))
+    grad[0] = adj + PRIOR_WEIGHT * (jnp.log(d[0]) - jnp.log(p[0]))
     copy_grad = pltpu.make_async_copy(grad, grad_hbm, sems.at[3])
     copy_grad.start()
     copy_res.wait()
@@ -303,10 +359,11 @@
         scratch_shapes=[
             *[pltpu.VMEM((layers, COMPS, 2 * BLOCK, RANK * LANES), BF16)] * 2,
             *[pltpu.VMEM((COMPS, padded, LANES), BF16)] * 2,
-            *[pltpu.VMEM((width, FILTERS * LANES), BF16)] * 2,
+            *[pltpu.VMEM((COMPS, width, RANK * LANES), BF16)] * 2,
             pltpu.VMEM((COMPS, rows, width), F32),
             pltpu.VMEM((COMPS, share, width), F32),
             *[pltpu.VMEM((1, rows, width), F32)] * 3,
+            pltpu.VMEM((width, 2 * LANES), F32),
             pltpu.SemaphoreType.DMA((4,)),
         ],
         compiler_params=limit(12 + 2 * layers),
@@ -317,21 +374,23 @@
 def body(density, prior, observed, filter_across, filter_along, comp_weight):
     layers, tiles = lax.axis_size("depth"), lax.axis_size("tile")
     both = ("depth", "tile")
-    at = lambda d, t: d * tiles + t
+    turns = [[(d, (d + s) % layers) for d in range(layers)] for s in range(layers)]
     inner = [(i, i ^ 1) for i in range(tiles)]
-    outer = [(at(d, i), at(d, i + 1)) for d in range(layers) for i in range(1, tiles - 1, 2)]
+    outer = [(i, i + 1) for i in range(1, tiles - 1, 2)]
     outer += [(j, i) for i, j in outer]
-    outer += [(at(d, t), at(d ^ 1, t)) for d in range(layers) for t in (0, tiles - 1)]
-    turns = [[(d, (d + s) % layers) for d in range(layers)] for s in range(1, layers)]
-
-    sent, e, o = pack(density, observed, filter_across, filter_along)
-    bodies = [sent] + [lax.ppermute(sent, "depth", turn) for turn in turns]
-    from_e = lax.ppermute(e, "tile", inner)
-    from_o = lax.ppermute(o, both, outer)
+
+    def outward(s):
+        pairs = [(d * tiles + i, e * tiles + j) for d, e in turns[s] for i, j in outer]
+        return pairs + [(d * tiles + t, (e if s else d ^ 1) * tiles + t) for d, e in turns[s] for t in (0, tiles - 1)]
+
+    sent, observed = turn(density, filter_across, filter_along, observed)
+    bodies = [sent] + [lax.ppermute(sent, "depth", pairs) for pairs in turns[1:]]
+    out, out_other, inside = outer_part(sent, observed)
+    from_o = lax.ppermute(out, both, outward(0))
+    halos = [lax.ppermute(out_other, both, outward(s)) for s in range(1, layers)]
     tf, zf, tb, zb, shi, slo, obst = own_part(sent, observed)
-    halo = jnp.concatenate([from_e[0:HALO], from_o[0:HALO]], axis=0)
-    halo, _ = lax.optimization_barrier((halo, obst))
-    halos = [lax.ppermute(halo, "depth", turn) for turn in turns]
+    inside, _ = lax.optimization_barrier((inside, obst))
+    from_e = lax.ppermute(inner_part(inside, bodies), "tile", inner)
     others = [other_part(received) for received in bodies[1:]]
     tfs, zfs, shis, slos = ([first] + [x[i] for x in others] for i, first in enumerate((tf, zf, shi, slo)))
     return tuple(

time: 19.7 us -> 17.3 us (0.88)
  the two profiles are of different devices: /device:TPU:0 before, /device:TPU:31 now
where the time goes in v1:
time: 17.3 us; the launch traced here: 17 us
  Pallas kernels  11.1 us (64%)
  starting transfers between devices  4.51 us (26%)
  between operations  0.71 us (4%)
  waiting for transfers between devices  0.66 us (4%)
    pallas_call x1, Pallas kernels, final_part(): pl.pallas_call(lambda *refs: final_kernel(layers, *refs), out_shape=[jax....  6.5 us
    ppermute x1, starting transfers between devices, body(): from_e = lax.ppermute(inner_part(inside, bodies), 'tile', inner)  2.69 us
    pallas_call x1, Pallas kernels, own_part(): pl.pallas_call(own_kernel, out_shape=out, in_specs=[VMEM, VMEM], out_spec...  1.94 us
    ppermute x1, starting transfers between devices, body(): from_o = lax.ppermute(out, both, outward(0))  1.3 us
    pallas_call x1, Pallas kernels, turn(): pl.pallas_call(turn_kernel, out_shape=[jax.ShapeDtypeStruct((density.shap...  1.27 us
    pallas_call x1, Pallas kernels, other_part(): pl.pallas_call(other_kernel, out_shape=[along, across, smoothed, smoothed...  1.14 us
    ppermute x1, waiting for transfers between devices, body(): lax.ppermute(sent, 'depth', pairs)  0.65 us
  transfers between devices with their start and end apart: 4, of which 1 were waited for; matrix products, arithmetic and copies ran while one was open for 0% of the time, Pallas kernels for 20%

profile of v1, /device:TPU:31, one launch (start us, length us, event | category | flops | bytes accessed | tf_op | source)
XLA Modules:
  0.0 17.0 jit_solution(18421653480132545422)
XLA Ops:
  0.6 1.3 %turn.1 = (f32[280,128]{1,0:T(8,128)S(1)}, f32[6,128,256]{2,1,0:T(8,128)S(1)}) custom-call(f32[1,128,256]{2,1,0:T(8,128)} %refs_0_.1, f32[1,6,4,33]{3,2,1,0:T(4,128)} %fa_hbm.1, f32[1,6,4,33]{3,2,1,0:T(4,128)} %fl_hbm.1, f32[6,128,256]{2,1,0:T(8,128)} %o_hbm.1), custom_call_target="tpu_custom_call" | custom-call | tf_op jit(solution)/shard_map/turn/pallas_call | solution.py:56
  1.9 0.3 %collective-permute-start = (f32[280,128]{1,0:T(8,128)S(1)}, f32[280,128]{1,0:T(8,128)S(1)}, u32[]{:S(2)}, u32[]{:S(2)}) collective-permute-start(f32[280,128]{1,0:T(8,128)S(1)} %get-tuple-element.19.body_ref.refs_1_.refs_8_), channel_id=1, source_target_pairs={{0,16},{16,0},{1,17},{17,1},{2,18},{18,2},{3,19},{19,3},{4,20},{20... | collective-permute-start | bytes 430088 | tf_op jit(solution)/shard_map/ppermute | solution.py:387
  2.2 0.2 %outer.1 = (f32[128,128]{1,0:T(8,128)S(1)}, f32[32,128]{1,0:T(8,128)S(1)}, f32[96,128]{1,0:T(8,128)S(1)}) custom-call(f32[280,128]{1,0:T(8,128)S(1)} %get-tuple-element.19.body_ref.refs_1_.refs_8_, f32[6,128,256]{2,1,0:T(8,128)S(1)} %get-tuple-element.20.o_ref), custom_call_target="tpu_custom_call" | custom-call | tf_op jit(solution)/shard_map/outer/pallas_call | solution.py:96
  2.5 1.3 %collective-permute-start.2 = (f32[128,128]{1,0:T(8,128)S(1)}, f32[128,128]{1,0:T(8,128)S(1)}, u32[]{:S(2)}, u32[]{:S(2)}) collective-permute-start(f32[128,128]{1,0:T(8,128)S(1)} %get-tuple-element.24), channel_id=1, source_target_pairs={{1,2},{3,4},{5,6},{7,8},{9,10},{11,12},{13,14},{2,1},{4,3},{6,5},{... | collective-permute-start | bytes 196616 | tf_op jit(solution)/shard_map/ppermute | solution.py:389
  3.8 0.2 %collective-permute-start.3 = (f32[32,128]{1,0:T(8,128)S(1)}, f32[32,128]{1,0:T(8,128)S(1)}, u32[]{:S(2)}, u32[]{:S(2)}) collective-permute-start(f32[32,128]{1,0:T(8,128)S(1)} %get-tuple-element.35), channel_id=1, source_target_pairs={{1,18},{3,20},{5,22},{7,24},{9,26},{11,28},{13,30},{2,17},{4,19},{... | collective-permute-start | bytes 49160 | tf_op jit(solution)/shard_map/ppermute | solution.py:390
  4.0 1.9 %own.1 = (bf16[768,256]{1,0:T(8,128)(2,1)S(1)}, bf16[3072,256]{1,0:T(8,128)(2,1)S(1)}, bf16[768,256]{1,0:T(8,128)(2,1)S(1)}, bf16[3072,256]{1,0:T(8,128)(2,1)S(1...) custom-call(f32[280,128]{1,0:T(8,128)S(1)} %get-tuple-element.19.body_ref.refs_1_., ...), custom_call_target="tpu_custom_call" | custom-call | flops 2000000000 | bytes 4000000 | tf_op jit(solution)/shard_map/own/pallas_call | solution.py:230
  5.9 0.7 %collective-permute-done.refs_2_.body_ref.refs_9_ = f32[280,128]{1,0:T(8,128)S(1)} collective-permute-done((f32[280,128]{1,0:T(8,128)S(1)}, f32[280,128]{1,0:T(8,128)S(1)}, u32[]{:S(2)}, u32[]{:S(2)}) %collective-permute-start) | collective-permute-done | bytes 143392 | tf_op jit(solution)/shard_map/ppermute | solution.py:387
  6.6 0.0 copy-start
  6.6 2.7 %collective-permute-start.1 = (f32[160,128]{1,0:T(8,128)S(1)}, f32[160,128]{1,0:T(8,128)S(1)}, u32[]{:S(2)}, u32[]{:S(2)}) collective-permute-start(f32[160,128]{1,0:T(8,128)S(1)} %inner.1), channel_id=1, source_target_pairs={{0,1},{1,0},{2,3},{3,2},{4,5},{5,4},{6,7},{7,6},{8,9},{9,8},{10,11... | collective-permute-start | bytes 245768 | tf_op jit(solution)/shard_map/ppermute | solution.py:393
  9.3 1.1 %other.1 = (bf16[768,256]{1,0:T(8,128)(2,1)S(1)}, bf16[3072,256]{1,0:T(8,128)(2,1)S(1)}, bf16[6,224,512]{2,1,0:T(8,128)(2,1)S(1)}, bf16[6,224,512]{2,1,0:T(8,128)(2,1)S(1)}) custom-call(f32[280,128]{1,0:T(8,128)S(1)} %collective-permute-done.refs_2_.body_ref.refs_9_), custom_call_target="tpu_custom_call" | custom-call | flops 2000000000 | bytes 4000000 | tf_op jit(solution)/shard_map/other/pallas_call | solution.py:245
  10.4 0.0 collective-permute-done.3.refs_18_
  10.5 0.0 collective-permute-done.2.refs_4_
  10.5 0.0 collective-permute-done.1.refs_3_
  10.5 0.0 copy-done
  10.5 6.5 %final.1 = (f32[1,128,256]{2,1,0:T(8,128)}, f32[6,64,256]{2,1,0:T(8,128)}) custom-call(f32[1,128,256]{2,1,0:T(8,128)} %refs_0_.1, f32[1,128,256]{2,1,0:T(8,128)} %refs_1_.1, f32[6]{0:T(128)S(1)} %copy-done, f32[160,128]{1,0:T(8,128)S(1)} %collective-permute-done.1.refs_3_, f32[128,128]{1,0:T(8,128)S(1)} %collective-permute-done.2.refs_4_, ...), custom_call_target="tpu_custom_call" | custom-call | tf_op jit(solution)/shard_map/final/pallas_call | solution.py:354
  (1 shorter events, 0.0 us)
Async XLA Ops:
  1.9 4.7 %collective-permute-start = (f32[280,128]{1,0:T(8,128)S(1)}, f32[280,128]{1,0:T(8,128)S(1)}, u32[]{:S(2)}, u32[]{:S(2)}) collective-permute-start(f32[280,128]{1,0:T(8,128)S(1)} %get-tuple-element.19.body_ref.refs_1_.refs_8_), channel_id=1, source_target_pairs={{0,16},{16,0},{1,17},{17,1},{2,18},{18,2},{3,19},{19,3},{4,20},{20... | collective-permute-start | bytes 430088 | tf_op jit(solution)/shard_map/ppermute | solution.py:387
  2.5 8.0 %collective-permute-start.2 = (f32[128,128]{1,0:T(8,128)S(1)}, f32[128,128]{1,0:T(8,128)S(1)}, u32[]{:S(2)}, u32[]{:S(2)}) collective-permute-start(f32[128,128]{1,0:T(8,128)S(1)} %get-tuple-element.24), channel_id=1, source_target_pairs={{1,2},{3,4},{5,6},{7,8},{9,10},{11,12},{13,14},{2,1},{4,3},{6,5},{... | collective-permute-start | bytes 196616 | tf_op jit(solution)/shard_map/ppermute | solution.py:389
  3.8 6.7 %collective-permute-start.3 = (f32[32,128]{1,0:T(8,128)S(1)}, f32[32,128]{1,0:T(8,128)S(1)}, u32[]{:S(2)}, u32[]{:S(2)}) collective-permute-start(f32[32,128]{1,0:T(8,128)S(1)} %get-tuple-element.35), channel_id=1, source_target_pairs={{1,18},{3,20},{5,22},{7,24},{9,26},{11,28},{13,30},{2,17},{4,19},{... | collective-permute-start | bytes 49160 | tf_op jit(solution)/shard_map/ppermute | solution.py:390
  6.6 3.9 %copy-start = (f32[6]{0:T(128)S(1)}, f32[6]{0:T(128)}, u32[]{:S(2)}) copy-start(f32[6]{0:T(128)} %refs_2_.1) | copy-start | bytes 76
  6.6 3.9 %collective-permute-start.1 = (f32[160,128]{1,0:T(8,128)S(1)}, f32[160,128]{1,0:T(8,128)S(1)}, u32[]{:S(2)}, u32[]{:S(2)}) collective-permute-start(f32[160,128]{1,0:T(8,128)S(1)} %inner.1), channel_id=1, source_target_pairs={{0,1},{1,0},{2,3},{3,2},{4,5},{5,4},{6,7},{7,6},{8,9},{9,8},{10,11... | collective-permute-start | bytes 245768 | tf_op jit(solution)/shard_map/ppermute | solution.py:393

commit v2 on v1

--- a/solution.py
+++ b/solution.py
@@ -19,7 +19,6 @@
 BF16 = jnp.bfloat16
 VMEM = pl.BlockSpec(memory_space=pltpu.VMEM)
 HBM = pl.BlockSpec(memory_space=pltpu.HBM)
-SMEM = pl.BlockSpec(memory_space=pltpu.SMEM)
 
 
 def split(x):
@@ -127,42 +126,44 @@
     )(edge, *bodies)
 
 
-def place(filters, first_tap, targets):
+def place(base, filters, first_tap, targets):
     tap = lax.broadcasted_iota(jnp.int32, (LANES, LANES), 0) - first_tap
     lane = lax.broadcasted_iota(jnp.int32, (LANES, LANES), 1)
     chosen = jnp.zeros((LANES, LANES), jnp.bool_)
     for target in targets(tap):
         chosen = chosen | (lane == target)
     chosen = (chosen & (tap >= 0) & (tap < TAPS)).astype(BF16)
-    return [jnp.dot(v, chosen, preferred_element_type=F32) for v in split(filters)]
-
-
-def along_blocks(base, filters, targets, dst):
-    for p, placed in enumerate(place(filters, ALONG_AT, targets)):
-        base[p] = placed
+    hi, lo = (jnp.dot(v, chosen, preferred_element_type=F32) for v in split(filters))
+    base[...] = hi + lo
+
+
+def along_blocks(base, dst):
     for f in range(FILTERS):
-        for p in range(2):
-            v = jnp.broadcast_to(base[p, f : f + 1, :], (BLOCK, LANES))
-            v = pltpu.roll(v, 0, 1, stride=1, stride_axis=0)
-            dst[BLOCK * f : BLOCK * (f + 1), LANES * p : LANES * (p + 1)] = v.astype(BF16)
-
-
-def across_blocks(base, filters, targets, dst):
-    for p, placed in enumerate(place(filters, 0, targets)):
-        base[p] = placed
+        v = jnp.broadcast_to(base[f : f + 1, :], (BLOCK, LANES))
+        v = pltpu.roll(v, 0, 1, stride=1, stride_axis=0)
+        for p, part in enumerate(split(v)):
+            dst[BLOCK * f : BLOCK * (f + 1), LANES * p : LANES * (p + 1)] = part
+
+
+def across_blocks(base, dst):
     row = lax.broadcasted_iota(jnp.int32, (LANES, LANES), 0)
     lane = lax.broadcasted_iota(jnp.int32, (LANES, LANES), 1)
     band = jnp.abs(row - lane) <= MARGIN
     for f in range(FILTERS):
-        for p in range(2):
-            v = jnp.broadcast_to(base[p, f : f + 1, :], (LANES, LANES))
-            v = pltpu.roll(v, 0, 1, stride=1, stride_axis=0)
-            dst[LANES * f : LANES * (f + 1), LANES * p : LANES * (p + 1)] = jnp.where(band, v, 0.0).astype(BF16)
-
-
-def forward_tables(base, filters, tf, zf):
-    along_blocks(base, filters, lambda k: (k, k + 64), tf)
-    across_blocks(base, filters, lambda k: ((MARGIN - k) & (LANES - 1),), zf)
+        v = jnp.broadcast_to(base[f : f + 1, :], (LANES, LANES))
+        v = jnp.where(band, pltpu.roll(v, 0, 1, stride=1, stride_axis=0), 0.0)
+        for p, part in enumerate(split(v)):
+            dst[LANES * f : LANES * (f + 1), LANES * p : LANES * (p + 1)] = part
+
+
+def forward_places(base, filters):
+    place(base.at[0], filters, ALONG_AT, lambda k: (k, k + 64))
+    place(base.at[1], filters, 0, lambda k: ((MARGIN - k) & (LANES - 1),))
+
+
+def backward_places(base, filters):
+    place(base.at[2], filters, ALONG_AT, lambda k: (TAPS - 1 - k, TAPS - 1 - k + 64))
+    place(base.at[3], filters, 0, lambda k: ((k - MARGIN) & (LANES - 1),))
 
 
 def stacked(windows):
@@ -201,25 +202,30 @@
 def own_kernel(body_ref, o_ref, tf, zf, tb, zb, shi, slo, obst, dhi, dlo, base):
     width = dhi.shape[0]
     filters = body_ref[width : width + FILTERS, :]
-    forward_tables(base, filters, tf, zf)
+    forward_places(base, filters)
+    backward_places(base, filters)
+    along_blocks(base.at[0], tf)
     smooth_inside(body_ref, dhi, dlo, tf, shi, slo)
-    along_blocks(base, filters, lambda k: (TAPS - 1 - k, TAPS - 1 - k + 64), tb)
-    across_blocks(base, filters, lambda k: ((k - MARGIN) & (LANES - 1),), zb)
+    across_blocks(base.at[1], zf)
+    along_blocks(base.at[2], tb)
+    across_blocks(base.at[3], zb)
     for c in range(COMPS):
         obst[c] = o_ref[c].T
 
 
 def other_kernel(body_ref, tf, zf, shi, slo, dhi, dlo, base):
     width = dhi.shape[0]
-    forward_tables(base, body_ref[width : width + FILTERS, :], tf, zf)
+    forward_places(base, body_ref[width : width + FILTERS, :])
+    along_blocks(base.at[0], tf)
     smooth_inside(body_ref, dhi, dlo, tf, shi, slo)
+    across_blocks(base.at[1], zf)
 
 
 def tables(width):
     along = jax.ShapeDtypeStruct((FILTERS * BLOCK, 2 * LANES), BF16)
     across = jax.ShapeDtypeStruct((FILTERS * LANES, 2 * LANES), BF16)
     smoothed = jax.ShapeDtypeStruct((COMPS, width - BLOCK, RANK * LANES), BF16)
-    scratch = [pltpu.VMEM((width, LANES), BF16)] * 2 + [pltpu.VMEM((2, FILTERS, LANES), F32)]
+    scratch = [pltpu.VMEM((width, LANES), BF16)] * 2 + [pltpu.VMEM((4, FILTERS, LANES), F32)]
     return along, across, smoothed, scratch
 
 
@@ -257,13 +263,15 @@
 def final_kernel(layers, *refs):
     it = iter(refs)
     take = lambda k: [next(it) for _ in range(k)]
-    d_hbm, p_hbm, w_ref, e_ref, o_ref, tb, zb, obst = take(8)
+    d_hbm, p_hbm, w_hbm, e_ref, o_ref, tb, zb, obst = take(8)
     bodies, tfs, zfs, shis, slos = (take(layers) for _ in range(5))
     halos = take(layers - 1)
     grad_hbm, res_hbm = take(2)
-    ehi, elo, rhi, rlo, bhi, blo, turned, res, d, p, grad, acc, sems = take(13)
+    ehi, elo, rhi, rlo, bhi, blo, turned, res, d, p, grad, acc, w_ref, sems = take(14)
     copy_d = pltpu.make_async_copy(d_hbm, d, sems.at[0])
     copy_p = pltpu.make_async_copy(p_hbm, p, sems.at[1])
+    copy_w = pltpu.make_async_copy(w_hbm, w_ref, sems.at[4])
+    copy_w.start()
     copy_d.start()
     copy_p.start()
     tile, tiles = lax.axis_index("tile"), lax.axis_size("tile")
@@ -284,6 +292,7 @@
         smooth(tfs[l][...], windows, [into(ehi.at[l], elo.at[l], 0), into(ehi.at[l], elo.at[l], BLOCK)])
 
     first_row = lax.axis_index("depth") * share
+    copy_w.wait()
 
     def forward(c):
         lhs, rhs = [], []
@@ -350,11 +359,11 @@
     rows, width = density.shape[1:]
     share = rows // layers
     padded = width + 2 * MARGIN
-    args = [*in_hbm(density, prior), weight, e, o, tb, zb, obst, *bodies, *tfs, *zfs, *shis, *slos, *halos]
+    args = [*in_hbm(density, prior, weight), e, o, tb, zb, obst, *bodies, *tfs, *zfs, *shis, *slos, *halos]
     return pl.pallas_call(
         lambda *refs: final_kernel(layers, *refs),
         out_shape=[jax.ShapeDtypeStruct((1, rows, width), F32), jax.ShapeDtypeStruct((COMPS, share, width), F32)],
-        in_specs=[HBM, HBM, SMEM] + [VMEM] * (len(args) - 3),
+        in_specs=[HBM] * 3 + [VMEM] * (len(args) - 3),
         out_specs=[HBM, HBM],
         scratch_shapes=[
             *[pltpu.VMEM((layers, COMPS, 2 * BLOCK, RANK * LANES), BF16)] * 2,
@@ -364,7 +373,8 @@
             pltpu.VMEM((COMPS, share, width), F32),
             *[pltpu.VMEM((1, rows, width), F32)] * 3,
             pltpu.VMEM((width, 2 * LANES), F32),
-            pltpu.SemaphoreType.DMA((4,)),
+            pltpu.SMEM(weight.shape, F32),
+            pltpu.SemaphoreType.DMA((5,)),
         ],
         compiler_params=limit(12 + 2 * layers),
         name="final",

time: 17.3 us -> 16.2 us (0.936)
  Pallas kernels: 11.1 us -> 9.92 us
    pallas_call x1, Pallas kernels: 6.5 us -> 5.38 us  [final_part(): pl.pallas_call(lambda *refs: final_kernel(layers, *refs), out_shape=[jax....]
  transfers between devices with their start and end apart: 4 -> 4, of which waited for: 1 -> 1; matrix products, arithmetic and copies ran while one was open for 0% -> 0% of each run, Pallas kernels for 20% -> 21%
where the time goes in v2:
time: 16.2 us; the launch traced here: 15.9 us
  Pallas kernels  9.92 us (61%)
  starting transfers between devices  4.51 us (28%)
  waiting for transfers between devices  0.76 us (5%)
  between operations  0.69 us (4%)
    pallas_call x1, Pallas kernels, final_part(): pl.pallas_call(lambda *refs: final_kernel(layers, *refs), out_shape=[jax....  5.38 us
    ppermute x1, starting transfers between devices, body(): from_e = lax.ppermute(inner_part(inside, bodies), 'tile', inner)  2.69 us
    pallas_call x1, Pallas kernels, own_part(): pl.pallas_call(own_kernel, out_shape=out, in_specs=[VMEM, VMEM], out_spec...  1.84 us
    ppermute x1, starting transfers between devices, body(): from_o = lax.ppermute(out, both, outward(0))  1.3 us
    pallas_call x1, Pallas kernels, turn(): pl.pallas_call(turn_kernel, out_shape=[jax.ShapeDtypeStruct((density.shap...  1.27 us
    pallas_call x1, Pallas kernels, other_part(): pl.pallas_call(other_kernel, out_shape=[along, across, smoothed, smoothed...  1.17 us
    ppermute x1, waiting for transfers between devices, body(): lax.ppermute(sent, 'depth', pairs)  0.75 us
  transfers between devices with their start and end apart: 4, of which 1 were waited for; matrix products, arithmetic and copies ran while one was open for 0% of the time, Pallas kernels for 21%

profile of v2, /device:TPU:31, one launch (start us, length us, event | category | flops | bytes accessed | tf_op | source)
XLA Modules:
  0.0 15.9 jit_solution(8599187506121041555)
XLA Ops:
  0.6 1.3 %turn.1 = (f32[280,128]{1,0:T(8,128)S(1)}, f32[6,128,256]{2,1,0:T(8,128)S(1)}) custom-call(f32[1,128,256]{2,1,0:T(8,128)} %refs_0_.1, f32[1,6,4,33]{3,2,1,0:T(4,128)} %fa_hbm.1, f32[1,6,4,33]{3,2,1,0:T(4,128)} %fl_hbm.1, f32[6,128,256]{2,1,0:T(8,128)} %o_hbm.1), custom_call_target="tpu_custom_call" | custom-call | tf_op jit(solution)/shard_map/turn/pallas_call | solution.py:55
  1.9 0.3 %collective-permute-start = (f32[280,128]{1,0:T(8,128)S(1)}, f32[280,128]{1,0:T(8,128)S(1)}, u32[]{:S(2)}, u32[]{:S(2)}) collective-permute-start(f32[280,128]{1,0:T(8,128)S(1)} %get-tuple-element.19.body_ref.refs_1_.refs_8_), channel_id=1, source_target_pairs={{0,16},{16,0},{1,17},{17,1},{2,18},{18,2},{3,19},{19,3},{4,20},{20... | collective-permute-start | bytes 430088 | tf_op jit(solution)/shard_map/ppermute | solution.py:397
  2.2 0.2 %outer.1 = (f32[128,128]{1,0:T(8,128)S(1)}, f32[32,128]{1,0:T(8,128)S(1)}, f32[96,128]{1,0:T(8,128)S(1)}) custom-call(f32[280,128]{1,0:T(8,128)S(1)} %get-tuple-element.19.body_ref.refs_1_.refs_8_, f32[6,128,256]{2,1,0:T(8,128)S(1)} %get-tuple-element.20.o_ref), custom_call_target="tpu_custom_call" | custom-call | tf_op jit(solution)/shard_map/outer/pallas_call | solution.py:95
  2.5 1.3 %collective-permute-start.2 = (f32[128,128]{1,0:T(8,128)S(1)}, f32[128,128]{1,0:T(8,128)S(1)}, u32[]{:S(2)}, u32[]{:S(2)}) collective-permute-start(f32[128,128]{1,0:T(8,128)S(1)} %get-tuple-element.24), channel_id=1, source_target_pairs={{1,2},{3,4},{5,6},{7,8},{9,10},{11,12},{13,14},{2,1},{4,3},{6,5},{... | collective-permute-start | bytes 196616 | tf_op jit(solution)/shard_map/ppermute | solution.py:399
  3.8 0.2 %collective-permute-start.3 = (f32[32,128]{1,0:T(8,128)S(1)}, f32[32,128]{1,0:T(8,128)S(1)}, u32[]{:S(2)}, u32[]{:S(2)}) collective-permute-start(f32[32,128]{1,0:T(8,128)S(1)} %get-tuple-element.35), channel_id=1, source_target_pairs={{1,18},{3,20},{5,22},{7,24},{9,26},{11,28},{13,30},{2,17},{4,19},{... | collective-permute-start | bytes 49160 | tf_op jit(solution)/shard_map/ppermute | solution.py:400
  4.0 1.8 %own.1 = (bf16[768,256]{1,0:T(8,128)(2,1)S(1)}, bf16[3072,256]{1,0:T(8,128)(2,1)S(1)}, bf16[768,256]{1,0:T(8,128)(2,1)S(1)}, bf16[3072,256]{1,0:T(8,128)(2,1)S(1...) custom-call(f32[280,128]{1,0:T(8,128)S(1)} %get-tuple-element.19.body_ref.refs_1_., ...), custom_call_target="tpu_custom_call" | custom-call | flops 2000000000 | bytes 4000000 | tf_op jit(solution)/shard_map/own/pallas_call | solution.py:236
  5.8 0.8 %collective-permute-done.refs_2_.body_ref.refs_9_ = f32[280,128]{1,0:T(8,128)S(1)} collective-permute-done((f32[280,128]{1,0:T(8,128)S(1)}, f32[280,128]{1,0:T(8,128)S(1)}, u32[]{:S(2)}, u32[]{:S(2)}) %collective-permute-start) | collective-permute-done | bytes 143392 | tf_op jit(solution)/shard_map/ppermute | solution.py:397
  6.6 2.7 %collective-permute-start.1 = (f32[160,128]{1,0:T(8,128)S(1)}, f32[160,128]{1,0:T(8,128)S(1)}, u32[]{:S(2)}, u32[]{:S(2)}) collective-permute-start(f32[160,128]{1,0:T(8,128)S(1)} %inner.1), channel_id=1, source_target_pairs={{0,1},{1,0},{2,3},{3,2},{4,5},{5,4},{6,7},{7,6},{8,9},{9,8},{10,11... | collective-permute-start | bytes 245768 | tf_op jit(solution)/shard_map/ppermute | solution.py:403
  9.3 1.2 %other.1 = (bf16[768,256]{1,0:T(8,128)(2,1)S(1)}, bf16[3072,256]{1,0:T(8,128)(2,1)S(1)}, bf16[6,224,512]{2,1,0:T(8,128)(2,1)S(1)}, bf16[6,224,512]{2,1,0:T(8,128)(2,1)S(1)}) custom-call(f32[280,128]{1,0:T(8,128)S(1)} %collective-permute-done.refs_2_.body_ref.refs_9_), custom_call_target="tpu_custom_call" | custom-call | flops 2000000000 | bytes 4000000 | tf_op jit(solution)/shard_map/other/pallas_call | solution.py:251
  10.5 0.0 collective-permute-done.3.refs_18_
  10.5 0.0 collective-permute-done.2.refs_4_
  10.5 0.0 collective-permute-done.1.refs_3_
  10.5 5.4 %final.1 = (f32[1,128,256]{2,1,0:T(8,128)}, f32[6,64,256]{2,1,0:T(8,128)}) custom-call(f32[1,128,256]{2,1,0:T(8,128)} %refs_0_.1, f32[1,128,256]{2,1,0:T(8,128)} %refs_1_.1, f32[6]{0:T(128)} %refs_2_.1, f32[160,128]{1,0:T(8,128)S(1)} %collective-permute-done.1.refs_3_, f32[128,128]{1,0:T(8,128)S(1)} %collective-permute-done.2.refs_4_, ...), custom_call_target="tpu_custom_call" | custom-call | tf_op jit(solution)/shard_map/final/pallas_call | solution.py:363
  (1 shorter events, 0.0 us)
Async XLA Ops:
  1.9 4.7 %collective-permute-start = (f32[280,128]{1,0:T(8,128)S(1)}, f32[280,128]{1,0:T(8,128)S(1)}, u32[]{:S(2)}, u32[]{:S(2)}) collective-permute-start(f32[280,128]{1,0:T(8,128)S(1)} %get-tuple-element.19.body_ref.refs_1_.refs_8_), channel_id=1, source_target_pairs={{0,16},{16,0},{1,17},{17,1},{2,18},{18,2},{3,19},{19,3},{4,20},{20... | collective-permute-start | bytes 430088 | tf_op jit(solution)/shard_map/ppermute | solution.py:397
  2.5 8.0 %collective-permute-start.2 = (f32[128,128]{1,0:T(8,128)S(1)}, f32[128,128]{1,0:T(8,128)S(1)}, u32[]{:S(2)}, u32[]{:S(2)}) collective-permute-start(f32[128,128]{1,0:T(8,128)S(1)} %get-tuple-element.24), channel_id=1, source_target_pairs={{1,2},{3,4},{5,6},{7,8},{9,10},{11,12},{13,14},{2,1},{4,3},{6,5},{... | collective-permute-start | bytes 196616 | tf_op jit(solution)/shard_map/ppermute | solution.py:399
  3.8 6.7 %collective-permute-start.3 = (f32[32,128]{1,0:T(8,128)S(1)}, f32[32,128]{1,0:T(8,128)S(1)}, u32[]{:S(2)}, u32[]{:S(2)}) collective-permute-start(f32[32,128]{1,0:T(8,128)S(1)} %get-tuple-element.35), channel_id=1, source_target_pairs={{1,18},{3,20},{5,22},{7,24},{9,26},{11,28},{13,30},{2,17},{4,19},{... | collective-permute-start | bytes 49160 | tf_op jit(solution)/shard_map/ppermute | solution.py:400
  6.6 3.9 %collective-permute-start.1 = (f32[160,128]{1,0:T(8,128)S(1)}, f32[160,128]{1,0:T(8,128)S(1)}, u32[]{:S(2)}, u32[]{:S(2)}) collective-permute-start(f32[160,128]{1,0:T(8,128)S(1)} %inner.1), channel_id=1, source_target_pairs={{0,1},{1,0},{2,3},{3,2},{4,5},{5,4},{6,7},{7,6},{8,9},{9,8},{10,11... | collective-permute-start | bytes 245768 | tf_op jit(solution)/shard_map/ppermute | solution.py:403

commit v3 on v2

--- a/solution.py
+++ b/solution.py
@@ -137,21 +137,24 @@
     base[...] = hi + lo
 
 
-def along_blocks(base, dst):
-    for f in range(FILTERS):
+def along_blocks(base, dst, chosen=range(FILTERS)):
+    for f in chosen:
         v = jnp.broadcast_to(base[f : f + 1, :], (BLOCK, LANES))
         v = pltpu.roll(v, 0, 1, stride=1, stride_axis=0)
         for p, part in enumerate(split(v)):
             dst[BLOCK * f : BLOCK * (f + 1), LANES * p : LANES * (p + 1)] = part
 
 
-def across_blocks(base, dst):
-    row = lax.broadcasted_iota(jnp.int32, (LANES, LANES), 0)
-    lane = lax.broadcasted_iota(jnp.int32, (LANES, LANES), 1)
-    band = jnp.abs(row - lane) <= MARGIN
-    for f in range(FILTERS):
+def across_blocks(base, dst, chosen=range(FILTERS)):
+    row = lax.broadcasted_iota(jnp.int32, (MARGIN, LANES), 0)
+    lane = lax.broadcasted_iota(jnp.int32, (MARGIN, LANES), 1)
+    head, tail = lane <= row + MARGIN, lane >= row + LANES - 2 * MARGIN
+    for f in chosen:
         v = jnp.broadcast_to(base[f : f + 1, :], (LANES, LANES))
-        v = jnp.where(band, pltpu.roll(v, 0, 1, stride=1, stride_axis=0), 0.0)
+        v = pltpu.roll(v, 0, 1, stride=1, stride_axis=0)
+        v = jnp.concatenate(
+            [jnp.where(head, v[:MARGIN], 0.0), v[MARGIN : LANES - MARGIN], jnp.where(tail, v[LANES - MARGIN :], 0.0)], axis=0
+        )
         for p, part in enumerate(split(v)):
             dst[LANES * f : LANES * (f + 1), LANES * p : LANES * (p + 1)] = part
 
@@ -189,36 +192,34 @@
     return store
 
 
-def smooth_inside(body_ref, dhi, dlo, tf, shi, slo):
+def forward_inside(body_ref, dhi, dlo, base, tf, zf, shi, slo):
     width = dhi.shape[0]
     dhi[...], dlo[...] = split(body_ref[0:width, :])
+    along_blocks(base.at[0], tf)
     inside = width // BLOCK - 1
     window = lambda b: (dhi[BLOCK * b : BLOCK * b + 64, :], dlo[BLOCK * b : BLOCK * b + 64, :])
-    for b in range(0, inside, 2):
+    starts = range(0, inside, 2)
+    for n, b in enumerate(starts):
         group = range(b, min(b + 2, inside))
         smooth(tf[...], [window(i) for i in group], [into(shi, slo, BLOCK * i) for i in group])
+        across_blocks(base.at[1], zf, range(n, FILTERS, len(starts)))
 
 
 def own_kernel(body_ref, o_ref, tf, zf, tb, zb, shi, slo, obst, dhi, dlo, base):
-    width = dhi.shape[0]
-    filters = body_ref[width : width + FILTERS, :]
+    filters = body_ref[dhi.shape[0] :, :]
     forward_places(base, filters)
     backward_places(base, filters)
-    along_blocks(base.at[0], tf)
-    smooth_inside(body_ref, dhi, dlo, tf, shi, slo)
-    across_blocks(base.at[1], zf)
-    along_blocks(base.at[2], tb)
-    across_blocks(base.at[3], zb)
+    forward_inside(body_ref, dhi, dlo, base, tf, zf, shi, slo)
     for c in range(COMPS):
+        chosen = range(RANK * c, RANK * (c + 1))
+        along_blocks(base.at[2], tb, chosen)
+        across_blocks(base.at[3], zb, chosen)
         obst[c] = o_ref[c].T
 
 
 def other_kernel(body_ref, tf, zf, shi, slo, dhi, dlo, base):
-    width = dhi.shape[0]
-    forward_places(base, body_ref[width : width + FILTERS, :])
-    along_blocks(base.at[0], tf)
-    smooth_inside(body_ref, dhi, dlo, tf, shi, slo)
-    across_blocks(base.at[1], zf)
+    forward_places(base, body_ref[dhi.shape[0] :, :])
+    forward_inside(body_ref, dhi, dlo, base, tf, zf, shi, slo)
 
 
 def tables(width):
@@ -317,7 +318,7 @@
         turned[c] = center.T
         res[c] = turned[c, pl.ds(first_row, share), :]
 
-    def adjoint(c):
+    def smooth_back(c):
         window = lambda b: (rhi[c, BLOCK * b : BLOCK * b + 64, :], rlo[c, BLOCK * b : BLOCK * b + 64, :])
 
         def store(b):
@@ -331,19 +332,24 @@
         table = tb[RANK * BLOCK * c : RANK * BLOCK * (c + 1), :]
         for b in range(0, width // BLOCK, 2):
             smooth(table, [window(b), window(b + 1)], [store(b), store(b + 1)])
+
+    def across(c):
         z = zb[RANK * LANES * c : RANK * LANES * (c + 1), :]
         return jnp.dot(jnp.concatenate([bhi[c], blo[c]], axis=1), jnp.concatenate([z, z], axis=0), preferred_element_type=F32)
 
-    for c in range(COMPS + 1):
+    for c in range(COMPS + 2):
         if c < COMPS:
             forward(c)
         if c == COMPS - 1:
             copy_res = pltpu.make_async_copy(res, res_hbm, sems.at[2])
             copy_res.start()
-        if c == 1:
-            acc[...] = adjoint(0)
-        if c > 1:
-            acc[...] += adjoint(c - 1)
+        if c == 3:
+            acc[...] = across(0)
+        if 3 < c:
+            acc[...] += across(c - 3)
+        if 1 < c:
+            smooth_back(c - 2)
+    acc[...] += across(COMPS - 1)
     out = acc[...]
     adj = (out[:, 0:LANES] + out[:, LANES : 2 * LANES]).T
     copy_d.wait()

time: 16.2 us -> 15.9 us (0.981)
  the two profiles are of different devices: /device:TPU:31 before, /device:TPU:3 now
where the time goes in v3:
time: 15.9 us; the launch traced here: 15.7 us
  Pallas kernels  9.6 us (60%)
  starting transfers between devices  4.18 us (26%)
  waiting for transfers between devices  1.23 us (8%)
  between operations  0.68 us (4%)
    pallas_call x1, Pallas kernels, final_part(): pl.pallas_call(lambda *refs: final_kernel(layers, *refs), out_shape=[jax....  5.08 us
    ppermute x1, starting transfers between devices, body(): from_o = lax.ppermute(out, both, outward(0))  2.17 us
    pallas_call x1, Pallas kernels, own_part(): pl.pallas_call(own_kernel, out_shape=out, in_specs=[VMEM, VMEM], out_spec...  1.85 us
    ppermute x1, starting transfers between devices, body(): lax.ppermute(sent, 'depth', pairs)  1.3 us
    pallas_call x1, Pallas kernels, turn(): pl.pallas_call(turn_kernel, out_shape=[jax.ShapeDtypeStruct((density.shap...  1.27 us
    ppermute x1, waiting for transfers between devices, body(): lax.ppermute(out_other, both, outward(s))  1.22 us
    pallas_call x1, Pallas kernels, other_part(): pl.pallas_call(other_kernel, out_shape=[along, across, smoothed, smoothed...  1.15 us
    ppermute x1, starting transfers between devices, body(): lax.ppermute(out_other, both, outward(s))  0.48 us
  transfers between devices with their start and end apart: 4, of which 1 were waited for; matrix products, arithmetic and copies ran while one was open for 0% of the time, Pallas kernels for 21%

profile of v3, /device:TPU:3, one launch (start us, length us, event | category | flops | bytes accessed | tf_op | source)
XLA Modules:
  0.0 15.7 jit_solution(16552931998635047850)
XLA Ops:
  0.6 1.3 %turn.1 = (f32[280,128]{1,0:T(8,128)S(1)}, f32[6,128,256]{2,1,0:T(8,128)S(1)}) custom-call(f32[1,128,256]{2,1,0:T(8,128)} %refs_0_.1, f32[1,6,4,33]{3,2,1,0:T(4,128)} %fa_hbm.1, f32[1,6,4,33]{3,2,1,0:T(4,128)} %fl_hbm.1, f32[6,128,256]{2,1,0:T(8,128)} %o_hbm.1), custom_call_target="tpu_custom_call" | custom-call | tf_op jit(solution)/shard_map/turn/pallas_call | solution.py:55
  1.9 1.3 %collective-permute-start = (f32[280,128]{1,0:T(8,128)S(1)}, f32[280,128]{1,0:T(8,128)S(1)}, u32[]{:S(2)}, u32[]{:S(2)}) collective-permute-start(f32[280,128]{1,0:T(8,128)S(1)} %get-tuple-element.19.body_ref.refs_1_.refs_8_), channel_id=1, source_target_pairs={{0,16},{16,0},{1,17},{17,1},{2,18},{18,2},{3,19},{19,3},{4,20},{20... | collective-permute-start | bytes 430088 | tf_op jit(solution)/shard_map/ppermute | solution.py:403
  3.2 0.2 %outer.1 = (f32[128,128]{1,0:T(8,128)S(1)}, f32[32,128]{1,0:T(8,128)S(1)}, f32[96,128]{1,0:T(8,128)S(1)}) custom-call(f32[280,128]{1,0:T(8,128)S(1)} %get-tuple-element.19.body_ref.refs_1_.refs_8_, f32[6,128,256]{2,1,0:T(8,128)S(1)} %get-tuple-element.20.o_ref), custom_call_target="tpu_custom_call" | custom-call | tf_op jit(solution)/shard_map/outer/pallas_call | solution.py:95
  3.5 2.2 %collective-permute-start.2 = (f32[128,128]{1,0:T(8,128)S(1)}, f32[128,128]{1,0:T(8,128)S(1)}, u32[]{:S(2)}, u32[]{:S(2)}) collective-permute-start(f32[128,128]{1,0:T(8,128)S(1)} %get-tuple-element.24), channel_id=1, source_target_pairs={{1,2},{3,4},{5,6},{7,8},{9,10},{11,12},{13,14},{2,1},{4,3},{6,5},{... | collective-permute-start | bytes 196616 | tf_op jit(solution)/shard_map/ppermute | solution.py:405
  5.6 0.5 %collective-permute-start.3 = (f32[32,128]{1,0:T(8,128)S(1)}, f32[32,128]{1,0:T(8,128)S(1)}, u32[]{:S(2)}, u32[]{:S(2)}) collective-permute-start(f32[32,128]{1,0:T(8,128)S(1)} %get-tuple-element.35), channel_id=1, source_target_pairs={{1,18},{3,20},{5,22},{7,24},{9,26},{11,28},{13,30},{2,17},{4,19},{... | collective-permute-start | bytes 49160 | tf_op jit(solution)/shard_map/ppermute | solution.py:406
  6.1 1.8 %own.1 = (bf16[768,256]{1,0:T(8,128)(2,1)S(1)}, bf16[3072,256]{1,0:T(8,128)(2,1)S(1)}, bf16[768,256]{1,0:T(8,128)(2,1)S(1)}, bf16[3072,256]{1,0:T(8,128)(2,1)S(1...) custom-call(f32[280,128]{1,0:T(8,128)S(1)} %get-tuple-element.19.body_ref.refs_1_., ...), custom_call_target="tpu_custom_call" | custom-call | flops 2000000000 | bytes 4000000 | tf_op jit(solution)/shard_map/own/pallas_call | solution.py:237
  8.0 0.0 collective-permute-done.refs_2_.body_ref.refs_9_
  8.0 0.2 %collective-permute-start.1 = (f32[160,128]{1,0:T(8,128)S(1)}, f32[160,128]{1,0:T(8,128)S(1)}, u32[]{:S(2)}, u32[]{:S(2)}) collective-permute-start(f32[160,128]{1,0:T(8,128)S(1)} %inner.1), channel_id=1, source_target_pairs={{0,1},{1,0},{2,3},{3,2},{4,5},{5,4},{6,7},{7,6},{8,9},{9,8},{10,11... | collective-permute-start | bytes 245768 | tf_op jit(solution)/shard_map/ppermute | solution.py:409
  8.2 1.1 %other.1 = (bf16[768,256]{1,0:T(8,128)(2,1)S(1)}, bf16[3072,256]{1,0:T(8,128)(2,1)S(1)}, bf16[6,224,512]{2,1,0:T(8,128)(2,1)S(1)}, bf16[6,224,512]{2,1,0:T(8,128)(2,1)S(1)}) custom-call(f32[280,128]{1,0:T(8,128)S(1)} %collective-permute-done.refs_2_.body_ref.refs_9_), custom_call_target="tpu_custom_call" | custom-call | flops 2000000000 | bytes 4000000 | tf_op jit(solution)/shard_map/other/pallas_call | solution.py:252
  9.4 1.2 %collective-permute-done.3.refs_18_ = f32[32,128]{1,0:T(8,128)S(1)} collective-permute-done((f32[32,128]{1,0:T(8,128)S(1)}, f32[32,128]{1,0:T(8,128)S(1)}, u32[]{:S(2)}, u32[]{:S(2)}) %collective-permute-start.3) | collective-permute-done | bytes 16416 | tf_op jit(solution)/shard_map/ppermute | solution.py:406
  10.6 0.0 collective-permute-done.2.refs_4_
  10.6 0.0 collective-permute-done.1.refs_3_
  10.6 5.1 %final.1 = (f32[1,128,256]{2,1,0:T(8,128)}, f32[6,64,256]{2,1,0:T(8,128)}) custom-call(f32[1,128,256]{2,1,0:T(8,128)} %refs_0_.1, f32[1,128,256]{2,1,0:T(8,128)} %refs_1_.1, f32[6]{0:T(128)} %refs_2_.1, f32[160,128]{1,0:T(8,128)S(1)} %collective-permute-done.1.refs_3_, f32[128,128]{1,0:T(8,128)S(1)} %collective-permute-done.2.refs_4_, ...), custom_call_target="tpu_custom_call" | custom-call | tf_op jit(solution)/shard_map/final/pallas_call | solution.py:369
  (1 shorter events, 0.0 us)
Async XLA Ops:
  1.9 6.1 %collective-permute-start = (f32[280,128]{1,0:T(8,128)S(1)}, f32[280,128]{1,0:T(8,128)S(1)}, u32[]{:S(2)}, u32[]{:S(2)}) collective-permute-start(f32[280,128]{1,0:T(8,128)S(1)} %get-tuple-element.19.body_ref.refs_1_.refs_8_), channel_id=1, source_target_pairs={{0,16},{16,0},{1,17},{17,1},{2,18},{18,2},{3,19},{19,3},{4,20},{20... | collective-permute-start | bytes 430088 | tf_op jit(solution)/shard_map/ppermute | solution.py:403
  3.5 7.1 %collective-permute-start.2 = (f32[128,128]{1,0:T(8,128)S(1)}, f32[128,128]{1,0:T(8,128)S(1)}, u32[]{:S(2)}, u32[]{:S(2)}) collective-permute-start(f32[128,128]{1,0:T(8,128)S(1)} %get-tuple-element.24), channel_id=1, source_target_pairs={{1,2},{3,4},{5,6},{7,8},{9,10},{11,12},{13,14},{2,1},{4,3},{6,5},{... | collective-permute-start | bytes 196616 | tf_op jit(solution)/shard_map/ppermute | solution.py:405
  5.6 5.0 %collective-permute-start.3 = (f32[32,128]{1,0:T(8,128)S(1)}, f32[32,128]{1,0:T(8,128)S(1)}, u32[]{:S(2)}, u32[]{:S(2)}) collective-permute-start(f32[32,128]{1,0:T(8,128)S(1)} %get-tuple-element.35), channel_id=1, source_target_pairs={{1,18},{3,20},{5,22},{7,24},{9,26},{11,28},{13,30},{2,17},{4,19},{... | collective-permute-start | bytes 49160 | tf_op jit(solution)/shard_map/ppermute | solution.py:406
  8.0 2.6 %collective-permute-start.1 = (f32[160,128]{1,0:T(8,128)S(1)}, f32[160,128]{1,0:T(8,128)S(1)}, u32[]{:S(2)}, u32[]{:S(2)}) collective-permute-start(f32[160,128]{1,0:T(8,128)S(1)} %inner.1), channel_id=1, source_target_pairs={{0,1},{1,0},{2,3},{3,2},{4,5},{5,4},{6,7},{7,6},{8,9},{9,8},{10,11... | collective-permute-start | bytes 245768 | tf_op jit(solution)/shard_map/ppermute | solution.py:409

commit v4 on v3

--- a/solution.py
+++ b/solution.py
@@ -78,12 +78,10 @@
     return jnp.where(is_even(), x[x.shape[0] - HALO : x.shape[0], :], x[0:HALO, :])
 
 
-def outer_kernel(body_ref, o_ref, out_ref, od_ref, in_ref):
+def outer_kernel(body_ref, o_ref, out_ref, in_ref):
     width = o_ref.shape[2]
     even = is_even()
-    edge = outer_edge(body_ref.at[0:width])
-    out_ref[0:HALO, :] = edge
-    od_ref[...] = edge
+    out_ref[0:HALO, :] = outer_edge(body_ref.at[0:width])
     for c in range(COMPS):
         first = o_ref[c, :, 0:LANES].T[0:MARGIN]
         last = o_ref[c, :, width - LANES : width].T[LANES - MARGIN : LANES]
@@ -91,16 +89,30 @@
         in_ref[MARGIN * c : MARGIN * (c + 1), :] = jnp.where(even, last, first)
 
 
+def cut_kernel(body_ref, od_ref):
+    od_ref[...] = outer_edge(body_ref.at[0 : body_ref.shape[0] - FILTERS])
+
+
+def cut_part(sent):
+    return pl.pallas_call(
+        cut_kernel,
+        out_shape=jax.ShapeDtypeStruct((HALO, LANES), F32),
+        in_specs=[VMEM],
+        out_specs=VMEM,
+        compiler_params=limit(4),
+        name="cut",
+    )(sent)
+
+
 def outer_part(sent, observed):
     return pl.pallas_call(
         outer_kernel,
         out_shape=[
             jax.ShapeDtypeStruct((HALO + COMPS * MARGIN, LANES), F32),
-            jax.ShapeDtypeStruct((HALO, LANES), F32),
             jax.ShapeDtypeStruct((COMPS * MARGIN, LANES), F32),
         ],
         in_specs=[VMEM] * 2,
-        out_specs=[VMEM] * 3,
+        out_specs=[VMEM] * 2,
         compiler_params=limit(4),
         name="outer",
     )(sent, observed)
@@ -340,7 +352,7 @@
     for c in range(COMPS + 2):
         if c < COMPS:
             forward(c)
-        if c == COMPS - 1:
+        if c == COMPS:
             copy_res = pltpu.make_async_copy(res, res_hbm, sems.at[2])
             copy_res.start()
         if c == 3:
@@ -401,7 +413,9 @@
 
     sent, observed = turn(density, filter_across, filter_along, observed)
     bodies = [sent] + [lax.ppermute(sent, "depth", pairs) for pairs in turns[1:]]
-    out, out_other, inside = outer_part(sent, observed)
+    out_other = cut_part(sent)
+    turned, _ = lax.optimization_barrier((sent, out_other))
+    out, inside = outer_part(turned, observed)
     from_o = lax.ppermute(out, both, outward(0))
     halos = [lax.ppermute(out_other, both, outward(s)) for s in range(1, layers)]
     tf, zf, tb, zb, shi, slo, obst = own_part(sent, observed)

time: 15.9 us -> 15.8 us (level)
  the two profiles are of different devices: /device:TPU:3 before, /device:TPU:31 now
where the time goes in v4:
time: 15.8 us; the launch traced here: 15.6 us
  Pallas kernels  9.64 us (61%)
  starting transfers between devices  4.49 us (28%)
  waiting for transfers between devices  0.77 us (5%)
  between operations  0.69 us (4%)
    pallas_call x1, Pallas kernels, final_part(): pl.pallas_call(lambda *refs: final_kernel(layers, *refs), out_shape=[jax....  5.11 us
    ppermute x1, starting transfers between devices, body(): from_e = lax.ppermute(inner_part(inside, bodies), 'tile', inner)  2.67 us
    pallas_call x1, Pallas kernels, own_part(): pl.pallas_call(own_kernel, out_shape=out, in_specs=[VMEM, VMEM], out_spec...  1.85 us
    pallas_call x1, Pallas kernels, turn(): pl.pallas_call(turn_kernel, out_shape=[jax.ShapeDtypeStruct((density.shap...  1.27 us
    ppermute x1, starting transfers between devices, body(): lax.ppermute(out_other, both, outward(s))  1.24 us
    pallas_call x1, Pallas kernels, other_part(): pl.pallas_call(other_kernel, out_shape=[along, across, smoothed, smoothed...  1.15 us
    ppermute x1, waiting for transfers between devices, body(): lax.ppermute(sent, 'depth', pairs)  0.76 us
  transfers between devices with their start and end apart: 4, of which 1 were waited for; matrix products, arithmetic and copies ran while one was open for 0% of the time, Pallas kernels for 21%

profile of v4, /device:TPU:31, one launch (start us, length us, event | category | flops | bytes accessed | tf_op | source)
XLA Modules:
  0.0 15.6 jit_solution(14894668632959328236)
XLA Ops:
  0.6 1.3 %turn.1 = (f32[280,128]{1,0:T(8,128)S(1)}, f32[6,128,256]{2,1,0:T(8,128)S(1)}) custom-call(f32[1,128,256]{2,1,0:T(8,128)} %refs_0_.1, f32[1,6,4,33]{3,2,1,0:T(4,128)} %fa_hbm.1, f32[1,6,4,33]{3,2,1,0:T(4,128)} %fl_hbm.1, f32[6,128,256]{2,1,0:T(8,128)} %o_hbm.1), custom_call_target="tpu_custom_call" | custom-call | tf_op jit(solution)/shard_map/turn/pallas_call | solution.py:55
  1.9 0.3 %collective-permute-start = (f32[280,128]{1,0:T(8,128)S(1)}, f32[280,128]{1,0:T(8,128)S(1)}, u32[]{:S(2)}, u32[]{:S(2)}) collective-permute-start(f32[280,128]{1,0:T(8,128)S(1)} %get-tuple-element.20.body_ref.refs_1_.refs_8_), channel_id=1, source_target_pairs={{0,16},{16,0},{1,17},{17,1},{2,18},{18,2},{3,19},{19,3},{4,20},{20... | collective-permute-start | bytes 430088 | tf_op jit(solution)/shard_map/ppermute | solution.py:415
  2.2 1.2 %collective-permute-start.3 = (f32[32,128]{1,0:T(8,128)S(1)}, f32[32,128]{1,0:T(8,128)S(1)}, u32[]{:S(2)}, u32[]{:S(2)}) collective-permute-start(f32[32,128]{1,0:T(8,128)S(1)} %cut.1), channel_id=1, source_target_pairs={{1,18},{3,20},{5,22},{7,24},{9,26},{11,28},{13,30},{2,17},{4,19},{... | collective-permute-start | bytes 49160 | tf_op jit(solution)/shard_map/ppermute | solution.py:420
  3.4 0.2 %outer.1 = (f32[128,128]{1,0:T(8,128)S(1)}, f32[96,128]{1,0:T(8,128)S(1)}) custom-call(f32[280,128]{1,0:T(8,128)S(1)} %get-tuple-element.20.body_ref.refs_1_.refs_8_, f32[6,128,256]{2,1,0:T(8,128)S(1)} %get-tuple-element.21.o_ref), custom_call_target="tpu_custom_call" | custom-call | tf_op jit(solution)/shard_map/outer/pallas_call | solution.py:108
  3.7 0.3 %collective-permute-start.2 = (f32[128,128]{1,0:T(8,128)S(1)}, f32[128,128]{1,0:T(8,128)S(1)}, u32[]{:S(2)}, u32[]{:S(2)}) collective-permute-start(f32[128,128]{1,0:T(8,128)S(1)} %get-tuple-element.25), channel_id=1, source_target_pairs={{1,2},{3,4},{5,6},{7,8},{9,10},{11,12},{13,14},{2,1},{4,3},{6,5},{... | collective-permute-start | bytes 196616 | tf_op jit(solution)/shard_map/ppermute | solution.py:419
  4.0 1.8 %own.1 = (bf16[768,256]{1,0:T(8,128)(2,1)S(1)}, bf16[3072,256]{1,0:T(8,128)(2,1)S(1)}, bf16[768,256]{1,0:T(8,128)(2,1)S(1)}, bf16[3072,256]{1,0:T(8,128)(2,1)S(1...) custom-call(f32[280,128]{1,0:T(8,128)S(1)} %get-tuple-element.20.body_ref.refs_1_., ...), custom_call_target="tpu_custom_call" | custom-call | flops 2000000000 | bytes 4000000 | tf_op jit(solution)/shard_map/own/pallas_call | solution.py:249
  5.8 0.8 %collective-permute-done.refs_2_.body_ref.refs_9_ = f32[280,128]{1,0:T(8,128)S(1)} collective-permute-done((f32[280,128]{1,0:T(8,128)S(1)}, f32[280,128]{1,0:T(8,128)S(1)}, u32[]{:S(2)}, u32[]{:S(2)}) %collective-permute-start) | collective-permute-done | bytes 143392 | tf_op jit(solution)/shard_map/ppermute | solution.py:415
  6.6 2.7 %collective-permute-start.1 = (f32[160,128]{1,0:T(8,128)S(1)}, f32[160,128]{1,0:T(8,128)S(1)}, u32[]{:S(2)}, u32[]{:S(2)}) collective-permute-start(f32[160,128]{1,0:T(8,128)S(1)} %inner.1), channel_id=1, source_target_pairs={{0,1},{1,0},{2,3},{3,2},{4,5},{5,4},{6,7},{7,6},{8,9},{9,8},{10,11... | collective-permute-start | bytes 245768 | tf_op jit(solution)/shard_map/ppermute | solution.py:423
  9.3 1.1 %other.1 = (bf16[768,256]{1,0:T(8,128)(2,1)S(1)}, bf16[3072,256]{1,0:T(8,128)(2,1)S(1)}, bf16[6,224,512]{2,1,0:T(8,128)(2,1)S(1)}, bf16[6,224,512]{2,1,0:T(8,128)(2,1)S(1)}) custom-call(f32[280,128]{1,0:T(8,128)S(1)} %collective-permute-done.refs_2_.body_ref.refs_9_), custom_call_target="tpu_custom_call" | custom-call | flops 2000000000 | bytes 4000000 | tf_op jit(solution)/shard_map/other/pallas_call | solution.py:264
  10.4 0.0 collective-permute-done.3.refs_18_
  10.4 0.0 collective-permute-done.2.refs_4_
  10.5 0.0 collective-permute-done.1.refs_3_
  10.5 5.1 %final.1 = (f32[1,128,256]{2,1,0:T(8,128)}, f32[6,64,256]{2,1,0:T(8,128)}) custom-call(f32[1,128,256]{2,1,0:T(8,128)} %refs_0_.1, f32[1,128,256]{2,1,0:T(8,128)} %refs_1_.1, f32[6]{0:T(128)} %refs_2_.1, f32[160,128]{1,0:T(8,128)S(1)} %collective-permute-done.1.refs_3_, f32[128,128]{1,0:T(8,128)S(1)} %collective-permute-done.2.refs_4_, ...), custom_call_target="tpu_custom_call" | custom-call | tf_op jit(solution)/shard_map/final/pallas_call | solution.py:381
  (2 shorter events, 0.0 us)
Async XLA Ops:
  1.9 4.7 %collective-permute-start = (f32[280,128]{1,0:T(8,128)S(1)}, f32[280,128]{1,0:T(8,128)S(1)}, u32[]{:S(2)}, u32[]{:S(2)}) collective-permute-start(f32[280,128]{1,0:T(8,128)S(1)} %get-tuple-element.20.body_ref.refs_1_.refs_8_), channel_id=1, source_target_pairs={{0,16},{16,0},{1,17},{17,1},{2,18},{18,2},{3,19},{19,3},{4,20},{20... | collective-permute-start | bytes 430088 | tf_op jit(solution)/shard_map/ppermute | solution.py:415
  2.2 8.2 %collective-permute-start.3 = (f32[32,128]{1,0:T(8,128)S(1)}, f32[32,128]{1,0:T(8,128)S(1)}, u32[]{:S(2)}, u32[]{:S(2)}) collective-permute-start(f32[32,128]{1,0:T(8,128)S(1)} %cut.1), channel_id=1, source_target_pairs={{1,18},{3,20},{5,22},{7,24},{9,26},{11,28},{13,30},{2,17},{4,19},{... | collective-permute-start | bytes 49160 | tf_op jit(solution)/shard_map/ppermute | solution.py:420
  3.7 6.8 %collective-permute-start.2 = (f32[128,128]{1,0:T(8,128)S(1)}, f32[128,128]{1,0:T(8,128)S(1)}, u32[]{:S(2)}, u32[]{:S(2)}) collective-permute-start(f32[128,128]{1,0:T(8,128)S(1)} %get-tuple-element.25), channel_id=1, source_target_pairs={{1,2},{3,4},{5,6},{7,8},{9,10},{11,12},{13,14},{2,1},{4,3},{6,5},{... | collective-permute-start | bytes 196616 | tf_op jit(solution)/shard_map/ppermute | solution.py:419
  6.6 3.8 %collective-permute-start.1 = (f32[160,128]{1,0:T(8,128)S(1)}, f32[160,128]{1,0:T(8,128)S(1)}, u32[]{:S(2)}, u32[]{:S(2)}) collective-permute-start(f32[160,128]{1,0:T(8,128)S(1)} %inner.1), channel_id=1, source_target_pairs={{0,1},{1,0},{2,3},{3,2},{4,5},{5,4},{6,7},{7,6},{8,9},{9,8},{10,11... | collective-permute-start | bytes 245768 | tf_op jit(solution)/shard_map/ppermute | solution.py:423

commit v5 on v4

--- a/solution.py
+++ b/solution.py
@@ -221,12 +221,13 @@
     filters = body_ref[dhi.shape[0] :, :]
     forward_places(base, filters)
     backward_places(base, filters)
+    for c in range(COMPS):
+        obst[c] = o_ref[c].T
     forward_inside(body_ref, dhi, dlo, base, tf, zf, shi, slo)
     for c in range(COMPS):
         chosen = range(RANK * c, RANK * (c + 1))
         along_blocks(base.at[2], tb, chosen)
         across_blocks(base.at[3], zb, chosen)
-        obst[c] = o_ref[c].T
 
 
 def other_kernel(body_ref, tf, zf, shi, slo, dhi, dlo, base):

time: 15.8 us -> 15.8 us (level)
  transfers between devices with their start and end apart: 4 -> 4, of which waited for: 1 -> 1; matrix products, arithmetic and copies ran while one was open for 0% -> 0% of each run, Pallas kernels for 21% -> 20%
where the time goes in v5:
time: 15.8 us; the launch traced here: 15.6 us
  Pallas kernels  9.5 us (60%)
  starting transfers between devices  4.49 us (28%)
  waiting for transfers between devices  0.91 us (6%)
  between operations  0.69 us (4%)
    pallas_call x1, Pallas kernels, final_part(): pl.pallas_call(lambda *refs: final_kernel(layers, *refs), out_shape=[jax....  5.11 us
    ppermute x1, starting transfers between devices, body(): from_e = lax.ppermute(inner_part(inside, bodies), 'tile', inner)  2.67 us
    pallas_call x1, Pallas kernels, own_part(): pl.pallas_call(own_kernel, out_shape=out, in_specs=[VMEM, VMEM], out_spec...  1.7 us
    pallas_call x1, Pallas kernels, turn(): pl.pallas_call(turn_kernel, out_shape=[jax.ShapeDtypeStruct((density.shap...  1.27 us
    ppermute x1, starting transfers between devices, body(): lax.ppermute(out_other, both, outward(s))  1.24 us
    pallas_call x1, Pallas kernels, other_part(): pl.pallas_call(other_kernel, out_shape=[along, across, smoothed, smoothed...  1.15 us
    ppermute x1, waiting for transfers between devices, body(): lax.ppermute(sent, 'depth', pairs)  0.9 us
  transfers between devices with their start and end apart: 4, of which 1 were waited for; matrix products, arithmetic and copies ran while one was open for 0% of the time, Pallas kernels for 20%

profile of v5, /device:TPU:31, one launch (start us, length us, event | category | flops | bytes accessed | tf_op | source)
XLA Modules:
  0.0 15.6 jit_solution(8747371424403939808)
XLA Ops:
  0.6 1.3 %turn.1 = (f32[280,128]{1,0:T(8,128)S(1)}, f32[6,128,256]{2,1,0:T(8,128)S(1)}) custom-call(f32[1,128,256]{2,1,0:T(8,128)} %refs_0_.1, f32[1,6,4,33]{3,2,1,0:T(4,128)} %fa_hbm.1, f32[1,6,4,33]{3,2,1,0:T(4,128)} %fl_hbm.1, f32[6,128,256]{2,1,0:T(8,128)} %o_hbm.1), custom_call_target="tpu_custom_call" | custom-call | tf_op jit(solution)/shard_map/turn/pallas_call | solution.py:55
  1.9 0.3 %collective-permute-start = (f32[280,128]{1,0:T(8,128)S(1)}, f32[280,128]{1,0:T(8,128)S(1)}, u32[]{:S(2)}, u32[]{:S(2)}) collective-permute-start(f32[280,128]{1,0:T(8,128)S(1)} %get-tuple-element.20.body_ref.refs_1_.refs_8_), channel_id=1, source_target_pairs={{0,16},{16,0},{1,17},{17,1},{2,18},{18,2},{3,19},{19,3},{4,20},{20... | collective-permute-start | bytes 430088 | tf_op jit(solution)/shard_map/ppermute | solution.py:416
  2.2 1.2 %collective-permute-start.3 = (f32[32,128]{1,0:T(8,128)S(1)}, f32[32,128]{1,0:T(8,128)S(1)}, u32[]{:S(2)}, u32[]{:S(2)}) collective-permute-start(f32[32,128]{1,0:T(8,128)S(1)} %cut.1), channel_id=1, source_target_pairs={{1,18},{3,20},{5,22},{7,24},{9,26},{11,28},{13,30},{2,17},{4,19},{... | collective-permute-start | bytes 49160 | tf_op jit(solution)/shard_map/ppermute | solution.py:421
  3.4 0.2 %outer.1 = (f32[128,128]{1,0:T(8,128)S(1)}, f32[96,128]{1,0:T(8,128)S(1)}) custom-call(f32[280,128]{1,0:T(8,128)S(1)} %get-tuple-element.20.body_ref.refs_1_.refs_8_, f32[6,128,256]{2,1,0:T(8,128)S(1)} %get-tuple-element.21.o_ref), custom_call_target="tpu_custom_call" | custom-call | tf_op jit(solution)/shard_map/outer/pallas_call | solution.py:108
  3.7 0.3 %collective-permute-start.2 = (f32[128,128]{1,0:T(8,128)S(1)}, f32[128,128]{1,0:T(8,128)S(1)}, u32[]{:S(2)}, u32[]{:S(2)}) collective-permute-start(f32[128,128]{1,0:T(8,128)S(1)} %get-tuple-element.25), channel_id=1, source_target_pairs={{1,2},{3,4},{5,6},{7,8},{9,10},{11,12},{13,14},{2,1},{4,3},{6,5},{... | collective-permute-start | bytes 196616 | tf_op jit(solution)/shard_map/ppermute | solution.py:420
  4.0 1.7 %own.1 = (bf16[768,256]{1,0:T(8,128)(2,1)S(1)}, bf16[3072,256]{1,0:T(8,128)(2,1)S(1)}, bf16[768,256]{1,0:T(8,128)(2,1)S(1)}, bf16[3072,256]{1,0:T(8,128)(2,1)S(1...) custom-call(f32[280,128]{1,0:T(8,128)S(1)} %get-tuple-element.20.body_ref.refs_1_., ...), custom_call_target="tpu_custom_call" | custom-call | flops 2000000000 | bytes 4000000 | tf_op jit(solution)/shard_map/own/pallas_call | solution.py:250
  5.7 0.9 %collective-permute-done.refs_2_.body_ref.refs_9_ = f32[280,128]{1,0:T(8,128)S(1)} collective-permute-done((f32[280,128]{1,0:T(8,128)S(1)}, f32[280,128]{1,0:T(8,128)S(1)}, u32[]{:S(2)}, u32[]{:S(2)}) %collective-permute-start) | collective-permute-done | bytes 143392 | tf_op jit(solution)/shard_map/ppermute | solution.py:416
  6.6 2.7 %collective-permute-start.1 = (f32[160,128]{1,0:T(8,128)S(1)}, f32[160,128]{1,0:T(8,128)S(1)}, u32[]{:S(2)}, u32[]{:S(2)}) collective-permute-start(f32[160,128]{1,0:T(8,128)S(1)} %inner.1), channel_id=1, source_target_pairs={{0,1},{1,0},{2,3},{3,2},{4,5},{5,4},{6,7},{7,6},{8,9},{9,8},{10,11... | collective-permute-start | bytes 245768 | tf_op jit(solution)/shard_map/ppermute | solution.py:424
  9.3 1.1 %other.1 = (bf16[768,256]{1,0:T(8,128)(2,1)S(1)}, bf16[3072,256]{1,0:T(8,128)(2,1)S(1)}, bf16[6,224,512]{2,1,0:T(8,128)(2,1)S(1)}, bf16[6,224,512]{2,1,0:T(8,128)(2,1)S(1)}) custom-call(f32[280,128]{1,0:T(8,128)S(1)} %collective-permute-done.refs_2_.body_ref.refs_9_), custom_call_target="tpu_custom_call" | custom-call | flops 2000000000 | bytes 4000000 | tf_op jit(solution)/shard_map/other/pallas_call | solution.py:265
  10.4 0.0 collective-permute-done.3.refs_18_
  10.4 0.0 collective-permute-done.2.refs_4_
  10.5 0.0 collective-permute-done.1.refs_3_
  10.5 5.1 %final.1 = (f32[1,128,256]{2,1,0:T(8,128)}, f32[6,64,256]{2,1,0:T(8,128)}) custom-call(f32[1,128,256]{2,1,0:T(8,128)} %refs_0_.1, f32[1,128,256]{2,1,0:T(8,128)} %refs_1_.1, f32[6]{0:T(128)} %refs_2_.1, f32[160,128]{1,0:T(8,128)S(1)} %collective-permute-done.1.refs_3_, f32[128,128]{1,0:T(8,128)S(1)} %collective-permute-done.2.refs_4_, ...), custom_call_target="tpu_custom_call" | custom-call | tf_op jit(solution)/shard_map/final/pallas_call | solution.py:382
  (2 shorter events, 0.0 us)
Async XLA Ops:
  1.9 4.7 %collective-permute-start = (f32[280,128]{1,0:T(8,128)S(1)}, f32[280,128]{1,0:T(8,128)S(1)}, u32[]{:S(2)}, u32[]{:S(2)}) collective-permute-start(f32[280,128]{1,0:T(8,128)S(1)} %get-tuple-element.20.body_ref.refs_1_.refs_8_), channel_id=1, source_target_pairs={{0,16},{16,0},{1,17},{17,1},{2,18},{18,2},{3,19},{19,3},{4,20},{20... | collective-permute-start | bytes 430088 | tf_op jit(solution)/shard_map/ppermute | solution.py:416
  2.2 8.2 %collective-permute-start.3 = (f32[32,128]{1,0:T(8,128)S(1)}, f32[32,128]{1,0:T(8,128)S(1)}, u32[]{:S(2)}, u32[]{:S(2)}) collective-permute-start(f32[32,128]{1,0:T(8,128)S(1)} %cut.1), channel_id=1, source_target_pairs={{1,18},{3,20},{5,22},{7,24},{9,26},{11,28},{13,30},{2,17},{4,19},{... | collective-permute-start | bytes 49160 | tf_op jit(solution)/shard_map/ppermute | solution.py:421
  3.7 6.8 %collective-permute-start.2 = (f32[128,128]{1,0:T(8,128)S(1)}, f32[128,128]{1,0:T(8,128)S(1)}, u32[]{:S(2)}, u32[]{:S(2)}) collective-permute-start(f32[128,128]{1,0:T(8,128)S(1)} %get-tuple-element.25), channel_id=1, source_target_pairs={{1,2},{3,4},{5,6},{7,8},{9,10},{11,12},{13,14},{2,1},{4,3},{6,5},{... | collective-permute-start | bytes 196616 | tf_op jit(solution)/shard_map/ppermute | solution.py:420
  6.6 3.8 %collective-permute-start.1 = (f32[160,128]{1,0:T(8,128)S(1)}, f32[160,128]{1,0:T(8,128)S(1)}, u32[]{:S(2)}, u32[]{:S(2)}) collective-permute-start(f32[160,128]{1,0:T(8,128)S(1)} %inner.1), channel_id=1, source_target_pairs={{0,1},{1,0},{2,3},{3,2},{4,5},{5,4},{6,7},{7,6},{8,9},{9,8},{10,11... | collective-permute-start | bytes 245768 | tf_op jit(solution)/shard_map/ppermute | solution.py:424
